TPU v7x, 32 devices: a whole 2x2x4 slice. The times are simulated.
32 devices in a mesh: gx: 2 (over y), gy: 4 (over x, core), gz: 4 (over z).
Axes of the slice: x: 2, y: 2, z: 4, core: 2. Of those that a mesh axis runs over, the one named last changes fastest.
Arguments:
- leaf_coeffs: float32 [512, 1000], P(('gx', 'gy', 'gz')), may hold values from -6 to 6
- operator_blocks: float32 [2, 7, 4, 3, 400], replicated, may hold values from -0.5 to 0.5
- term_ranks: int32 [2, 7], replicated, may hold values from 2 to 4
- target_device: int32 [64, 7, 1], P(('gx', 'gy', 'gz')), may hold values from 0 to 15; in each aligned block of 14 rows (0 to 13, 14 to 27, ..., all dimensions but the last counted through in order) at most 2 rows name the same one
- target_slot: int32 [64, 7], P(('gx', 'gy', 'gz')), may hold values from 0 to 1
- coarse_targets: int32 [16, 7], P(('gx', 'gy')), may hold values from 0 to 15
- parent_place: int32 [8, 8], P(('gx', 'gy')), may hold values from 0 to 15, as said below
Outputs:
- leaf_result: float32 [512, 1000], P(('gx', 'gy', 'gz'))
Inputs may be any that keep to these rules, and one draw needn't show every extreme that they name: `parent_place`: each row names distinct values. `target_device`: among the rows of one device, no value is named more than 2 times.
All inputs are finite; a program needn't handle non-finite values.
Results may differ from a plain program's by a relative error of at most 0.0003.
Values sent between devices are 32-bit elements; how exact they have to be, the bound alone decides.
A program may use at most 64 MiB of HBM per device.

v0:
```python
import jax
import jax.numpy as jnp
from jax import lax
from jax.sharding import PartitionSpec as P

ORDER = 10


precise = lax.Precision.HIGHEST


def two_scale(edge_len):
    row_index = jnp.arange(edge_len)[:, None].astype(jnp.float32)
    col_index = jnp.arange(edge_len)[None, :].astype(jnp.float32)
    filter_table = jnp.sqrt(2.0 / edge_len) * jnp.cos(
        jnp.pi * (col_index + 0.5) * row_index / edge_len
    )
    return jnp.where(row_index == 0, filter_table * jnp.sqrt(0.5), filter_table)


def transform(blocks, filter_table, inverse):
    if inverse:
        filter_table = filter_table.T
    return jnp.einsum(
        "ix,jy,kz,nxyz->nijk", filter_table, filter_table, filter_table, blocks, precision=precise
    )


def assemble(leaf_rows, order_len):
    node_count = leaf_rows.shape[0] // 8
    shaped = leaf_rows.reshape(node_count, 2, 2, 2, order_len, order_len, order_len)
    return shaped.transpose(0, 1, 4, 2, 5, 3, 6).reshape(
        node_count, 2 * order_len, 2 * order_len, 2 * order_len
    )


def split_octants(blocks, order_len):
    node_count = blocks.shape[0]
    shaped = blocks.reshape(node_count, 2, order_len, 2, order_len, 2, order_len)
    return shaped.transpose(0, 1, 3, 5, 2, 4, 6).reshape(node_count * 8, order_len**3)


def contributions(blocks, matrices, ranks, destination, buffer_rows):
    node_count, edge_len = (blocks.shape[0], blocks.shape[1])
    flattened = blocks.reshape(node_count, edge_len, edge_len * edge_len)
    term_count = matrices.shape[1]

    def per_disp(carry, entries):
        matrix_set, rank_now, target = entries
        kept_terms = (jnp.arange(term_count, dtype=jnp.int32) < rank_now).astype(jnp.float32)
        first_factor = (
            matrix_set[:, 0].reshape(term_count, edge_len, edge_len) * kept_terms[:, None, None]
        )
        second_factor = matrix_set[:, 1].reshape(term_count, edge_len, edge_len)
        third_factor = matrix_set[:, 2].reshape(term_count, edge_len, edge_len)
        partial_value = jnp.einsum("tia,nak->tnik", first_factor, flattened, precision=precise)
        partial_value = partial_value.reshape(term_count, node_count, edge_len, edge_len, edge_len)
        partial_value = jnp.einsum(
            "tjb,tnibc->tnjic", second_factor, partial_value, precision=precise
        )
        result = jnp.einsum("tkc,tnjic->nijk", third_factor, partial_value, precision=precise)
        return (carry, result.reshape(node_count, edge_len**3))

    _, pieces = lax.scan(per_disp, jnp.zeros((), jnp.float32), (matrices, ranks, destination.T))
    picker = (
        jnp.arange(buffer_rows, dtype=jnp.int32)[:, None] == destination.T.reshape(1, -1)
    ).astype(jnp.float32)
    return jnp.dot(
        picker,
        pieces.reshape(-1, edge_len**3),
        precision=precise,
        preferred_element_type=jnp.float32,
    )


def on_device(
    leaf_coeffs,
    operator_blocks,
    term_ranks,
    target_device,
    target_slot,
    coarse_targets,
    parent_place,
):
    edge_len = 2 * ORDER
    cell_count = edge_len**3
    filter_table = two_scale(edge_len)
    node_count = leaf_coeffs.shape[0] // 8
    coarse_count = coarse_targets.shape[0]
    middle_blocks = transform(assemble(leaf_coeffs, ORDER), filter_table, False)
    count_gy = lax.axis_size("gy")
    count_gz = lax.axis_size("gz")
    destination = target_device[:, :, 0] * node_count + target_slot
    middle_buffer = contributions(
        middle_blocks,
        operator_blocks[1],
        term_ranks[1],
        destination,
        count_gy * count_gz * node_count,
    )
    received = lax.all_to_all(middle_buffer, ("gy", "gz"), split_axis=0, concat_axis=0, tiled=True)
    middle_applied = jnp.sum(received.reshape(-1, node_count, cell_count), axis=0)
    corner_parts = middle_blocks[:, :ORDER, :ORDER, :ORDER].reshape(node_count, ORDER**3)
    column = lax.all_gather(corner_parts, "gz", axis=0, tiled=True)
    slot_index = jnp.arange(coarse_count * 8, dtype=jnp.int32)[:, None]
    picker = (slot_index == parent_place[0][None, :]).astype(jnp.float32)
    octants = jnp.dot(picker, column, precision=precise, preferred_element_type=jnp.float32)
    coarse_blocks = transform(assemble(octants, ORDER), filter_table, False)
    buffer_rows = lax.axis_size("gx") * lax.axis_size("gy") * coarse_count
    coarse_buffer = contributions(
        coarse_blocks, operator_blocks[0], term_ranks[0], coarse_targets, buffer_rows
    )
    arrived = lax.all_to_all(coarse_buffer, ("gx", "gy"), split_axis=0, concat_axis=0, tiled=True)
    coarse_applied = jnp.sum(arrived.reshape(-1, coarse_count, cell_count), axis=0)
    coarse_back = split_octants(
        transform(
            coarse_applied.reshape(coarse_count, edge_len, edge_len, edge_len), filter_table, True
        ),
        ORDER,
    )
    own_picker = lax.dynamic_slice_in_dim(picker, lax.axis_index("gz") * node_count, node_count, 1)
    from_parent = jnp.dot(
        own_picker.T, coarse_back, precision=precise, preferred_element_type=jnp.float32
    )
    middle_total = middle_applied.reshape(node_count, edge_len, edge_len, edge_len)
    middle_total = middle_total.at[:, :ORDER, :ORDER, :ORDER].add(
        from_parent.reshape(node_count, ORDER, ORDER, ORDER)
    )
    return split_octants(transform(middle_total, filter_table, True), ORDER)


def solution(mesh):
    in_specs = (
        P(("gx", "gy", "gz"), None),
        P(),
        P(),
        P(("gx", "gy", "gz"), None, None),
        P(("gx", "gy", "gz"), None),
        P(("gx", "gy"), None),
        P(("gx", "gy"), None),
    )
    out_specs = P(("gx", "gy", "gz"), None)
    return jax.shard_map(
        on_device, mesh=mesh, in_specs=in_specs, out_specs=out_specs, check_vma=False
    )
```

profile of v0, /device:TPU:0, one launch (start us, length us, event | category | flops | bytes accessed | tf_op | source)
XLA Modules:
  0.0 274.0 jit_solution(6364945980671598681)
XLA Ops:
  8.3 14.9 %all-gather = f32[4,2,1000]{2,1,0:T(2,128)S(1)} all-gather(f32[1,2,1000]{2,1,0:T(2,128)S(1)} %reshape.191), channel_id=1, replica_groups=mesh['gx'=2,'gy'=4,'gz'=4] {'gz'}, dimensions={0}, use_global_device_ids=true | all-gather | bytes 40000 | tf_op jit(solution)/shard_map/all_gather | solution.py:104
  31.2 96.7 %while.22 = (s32[]{:T(128)}, f32[7,2,8000]{2,1,0:T(2,128)S(1)}, f32[7,4,3,400]{3,1,2,0:T(4,128)}, s32[7]{0:T(128)}, f32[2,20,400]{2,1,0:T(8,128)S(1)}, /*index=5*/s32[]{:T(128)}) while((s32[]{:T(128)}, f32[7,2,8000]{2,1,0:T(2,128)S(1)}, f32[7,4,3,400]{3,1,2,0:T(4,128)}, s32[7]{0:T(128)}, f32[2,20,400]{2,1,0:T(8,128)S(1)}, ...), condition=%wide.region_4.5_spmd, body=%wide.region_3.4_spmd.sunk | while | flops 46081608 | bytes 2055557 | solution.py:64
  36.6 4.8 %fusion.221 = f32[4,2,20,20,20]{4,3,2,1,0:T(8,128)S(1)} fusion(f32[4,2,20,20,20]{4,3,2,1,0:T(8,128)} %reshape.230, f32[4,20,20,1,1]{2,1,0,3,4:T(8,128)S(1)} %reshape.231), kind=kOutput, calls=%fused_computation.21.clone.1 | convolution fusion | flops 15360000 | bytes 518400 | tf_op jit(solution)/shard_map/while/body/eval_jaxpr/tjb,tnibc->tnjic/dot_general | solution.py:58
  41.5 3.2 %fusion.222 = f32[2,20,20,20]{3,2,1,0:T(8,128)S(1)} fusion(f32[4,2,20,20,20]{4,3,2,1,0:T(8,128)S(1)} %fusion.221, f32[4,20,20,1,1]{2,1,0,3,4:T(8,128)S(1)} %reshape.232), kind=kOutput, calls=%fused_computation.16.clone.1 | convolution fusion | flops 15360000 | bytes 326400 | tf_op jit(solution)/shard_map/while/body/eval_jaxpr/tkc,tnjic->nijk/dot_general | solution.py:61
  50.4 4.8 %fusion.221 = f32[4,2,20,20,20]{4,3,2,1,0:T(8,128)S(1)} fusion(f32[4,2,20,20,20]{4,3,2,1,0:T(8,128)} %reshape.230, f32[4,20,20,1,1]{2,1,0,3,4:T(8,128)S(1)} %reshape.231), kind=kOutput, calls=%fused_computation.21.clone.1 | convolution fusion | flops 15360000 | bytes 518400 | tf_op jit(solution)/shard_map/while/body/eval_jaxpr/tjb,tnibc->tnjic/dot_general | solution.py:58
  55.3 3.2 %fusion.222 = f32[2,20,20,20]{3,2,1,0:T(8,128)S(1)} fusion(f32[4,2,20,20,20]{4,3,2,1,0:T(8,128)S(1)} %fusion.221, f32[4,20,20,1,1]{2,1,0,3,4:T(8,128)S(1)} %reshape.232), kind=kOutput, calls=%fused_computation.16.clone.1 | convolution fusion | flops 15360000 | bytes 326400 | tf_op jit(solution)/shard_map/while/body/eval_jaxpr/tkc,tnjic->nijk/dot_general | solution.py:61
  64.2 4.8 %fusion.221 = f32[4,2,20,20,20]{4,3,2,1,0:T(8,128)S(1)} fusion(f32[4,2,20,20,20]{4,3,2,1,0:T(8,128)} %reshape.230, f32[4,20,20,1,1]{2,1,0,3,4:T(8,128)S(1)} %reshape.231), kind=kOutput, calls=%fused_computation.21.clone.1 | convolution fusion | flops 15360000 | bytes 518400 | tf_op jit(solution)/shard_map/while/body/eval_jaxpr/tjb,tnibc->tnjic/dot_general | solution.py:58
  69.0 3.2 %fusion.222 = f32[2,20,20,20]{3,2,1,0:T(8,128)S(1)} fusion(f32[4,2,20,20,20]{4,3,2,1,0:T(8,128)S(1)} %fusion.221, f32[4,20,20,1,1]{2,1,0,3,4:T(8,128)S(1)} %reshape.232), kind=kOutput, calls=%fused_computation.16.clone.1 | convolution fusion | flops 15360000 | bytes 326400 | tf_op jit(solution)/shard_map/while/body/eval_jaxpr/tkc,tnjic->nijk/dot_general | solution.py:61
  78.0 4.8 %fusion.221 = f32[4,2,20,20,20]{4,3,2,1,0:T(8,128)S(1)} fusion(f32[4,2,20,20,20]{4,3,2,1,0:T(8,128)} %reshape.230, f32[4,20,20,1,1]{2,1,0,3,4:T(8,128)S(1)} %reshape.231), kind=kOutput, calls=%fused_computation.21.clone.1 | convolution fusion | flops 15360000 | bytes 518400 | tf_op jit(solution)/shard_map/while/body/eval_jaxpr/tjb,tnibc->tnjic/dot_general | solution.py:58
  82.8 3.2 %fusion.222 = f32[2,20,20,20]{3,2,1,0:T(8,128)S(1)} fusion(f32[4,2,20,20,20]{4,3,2,1,0:T(8,128)S(1)} %fusion.221, f32[4,20,20,1,1]{2,1,0,3,4:T(8,128)S(1)} %reshape.232), kind=kOutput, calls=%fused_computation.16.clone.1 | convolution fusion | flops 15360000 | bytes 326400 | tf_op jit(solution)/shard_map/while/body/eval_jaxpr/tkc,tnjic->nijk/dot_general | solution.py:61
  91.8 4.8 %fusion.221 = f32[4,2,20,20,20]{4,3,2,1,0:T(8,128)S(1)} fusion(f32[4,2,20,20,20]{4,3,2,1,0:T(8,128)} %reshape.230, f32[4,20,20,1,1]{2,1,0,3,4:T(8,128)S(1)} %reshape.231), kind=kOutput, calls=%fused_computation.21.clone.1 | convolution fusion | flops 15360000 | bytes 518400 | tf_op jit(solution)/shard_map/while/body/eval_jaxpr/tjb,tnibc->tnjic/dot_general | solution.py:58
  105.6 4.8 %fusion.221 = f32[4,2,20,20,20]{4,3,2,1,0:T(8,128)S(1)} fusion(f32[4,2,20,20,20]{4,3,2,1,0:T(8,128)} %reshape.230, f32[4,20,20,1,1]{2,1,0,3,4:T(8,128)S(1)} %reshape.231), kind=kOutput, calls=%fused_computation.21.clone.1 | convolution fusion | flops 15360000 | bytes 518400 | tf_op jit(solution)/shard_map/while/body/eval_jaxpr/tjb,tnibc->tnjic/dot_general | solution.py:58
  110.4 3.2 %fusion.222 = f32[2,20,20,20]{3,2,1,0:T(8,128)S(1)} fusion(f32[4,2,20,20,20]{4,3,2,1,0:T(8,128)S(1)} %fusion.221, f32[4,20,20,1,1]{2,1,0,3,4:T(8,128)S(1)} %reshape.232), kind=kOutput, calls=%fused_computation.16.clone.1 | convolution fusion | flops 15360000 | bytes 326400 | tf_op jit(solution)/shard_map/while/body/eval_jaxpr/tkc,tnjic->nijk/dot_general | solution.py:61
  119.3 4.8 %fusion.221 = f32[4,2,20,20,20]{4,3,2,1,0:T(8,128)S(1)} fusion(f32[4,2,20,20,20]{4,3,2,1,0:T(8,128)} %reshape.230, f32[4,20,20,1,1]{2,1,0,3,4:T(8,128)S(1)} %reshape.231), kind=kOutput, calls=%fused_computation.21.clone.1 | convolution fusion | flops 15360000 | bytes 518400 | tf_op jit(solution)/shard_map/while/body/eval_jaxpr/tjb,tnibc->tnjic/dot_general | solution.py:58
  124.2 3.2 %fusion.222 = f32[2,20,20,20]{3,2,1,0:T(8,128)S(1)} fusion(f32[4,2,20,20,20]{4,3,2,1,0:T(8,128)S(1)} %fusion.221, f32[4,20,20,1,1]{2,1,0,3,4:T(8,128)S(1)} %reshape.232), kind=kOutput, calls=%fused_computation.16.clone.1 | convolution fusion | flops 15360000 | bytes 326400 | tf_op jit(solution)/shard_map/while/body/eval_jaxpr/tkc,tnjic->nijk/dot_general | solution.py:61
  131.2 4.1 %all-to-all-start.1 = ((f32[8,2,8000]{2,1,0:T(2,128)}), f32[8,2,8000]{2,1,0:T(2,128)}, u32[]{:S(2)}, u32[]{:S(2)}) async-start(f32[8,2,8000]{2,1,0:T(2,128)} %copy.52), calls=%async_computation.1 | async-start | bytes 1032192 | tf_op jit(solution)/shard_map/all_to_all | solution.py:113
  135.7 90.9 %while.21 = (s32[]{:T(128)}, f32[7,2,8000]{2,1,0:T(2,128)S(1)}, f32[7,4,3,400]{3,1,2,0:T(4,128)}, s32[7]{0:T(128)S(1)}, f32[2,20,400]{2,1,0:T(8,128)S(1)}, /*index=5*/s32[]{:T(128)}) while((s32[]{:T(128)}, f32[7,2,8000]{2,1,0:T(2,128)S(1)}, f32[7,4,3,400]{3,1,2,0:T(4,128)}, s32[7]{0:T(128)S(1)}, f32[2,20,400]{2,1,0:T(8,128)S(1)}, ...), condition=%wide.region_1.2_spmd, body=%wide.region_0.1_spmd.sunk | while | flops 46081608 | bytes 2055557 | solution.py:64
  140.3 4.8 %fusion.212 = f32[4,2,20,20,20]{4,3,2,1,0:T(8,128)S(1)} fusion(f32[4,2,20,20,20]{4,3,2,1,0:T(8,128)} %reshape.227, f32[4,20,20,1,1]{2,1,0,3,4:T(8,128)S(1)} %reshape.228), kind=kOutput, calls=%fused_computation.7.clone.1 | convolution fusion | flops 15360000 | bytes 518400 | tf_op jit(solution)/shard_map/while/body/eval_jaxpr/tjb,tnibc->tnjic/dot_general | solution.py:58
  145.2 3.2 %fusion.213 = f32[2,20,20,20]{3,2,1,0:T(8,128)S(1)} fusion(f32[4,2,20,20,20]{4,3,2,1,0:T(8,128)S(1)} %fusion.212, f32[4,20,20,1,1]{2,1,0,3,4:T(8,128)S(1)} %reshape.229), kind=kOutput, calls=%fused_computation.2.clone.1 | convolution fusion | flops 15360000 | bytes 326400 | tf_op jit(solution)/shard_map/while/body/eval_jaxpr/tkc,tnjic->nijk/dot_general | solution.py:61
  153.3 4.8 %fusion.212 = f32[4,2,20,20,20]{4,3,2,1,0:T(8,128)S(1)} fusion(f32[4,2,20,20,20]{4,3,2,1,0:T(8,128)} %reshape.227, f32[4,20,20,1,1]{2,1,0,3,4:T(8,128)S(1)} %reshape.228), kind=kOutput, calls=%fused_computation.7.clone.1 | convolution fusion | flops 15360000 | bytes 518400 | tf_op jit(solution)/shard_map/while/body/eval_jaxpr/tjb,tnibc->tnjic/dot_general | solution.py:58
  158.2 3.2 %fusion.213 = f32[2,20,20,20]{3,2,1,0:T(8,128)S(1)} fusion(f32[4,2,20,20,20]{4,3,2,1,0:T(8,128)S(1)} %fusion.212, f32[4,20,20,1,1]{2,1,0,3,4:T(8,128)S(1)} %reshape.229), kind=kOutput, calls=%fused_computation.2.clone.1 | convolution fusion | flops 15360000 | bytes 326400 | tf_op jit(solution)/shard_map/while/body/eval_jaxpr/tkc,tnjic->nijk/dot_general | solution.py:61
  166.3 4.8 %fusion.212 = f32[4,2,20,20,20]{4,3,2,1,0:T(8,128)S(1)} fusion(f32[4,2,20,20,20]{4,3,2,1,0:T(8,128)} %reshape.227, f32[4,20,20,1,1]{2,1,0,3,4:T(8,128)S(1)} %reshape.228), kind=kOutput, calls=%fused_computation.7.clone.1 | convolution fusion | flops 15360000 | bytes 518400 | tf_op jit(solution)/shard_map/while/body/eval_jaxpr/tjb,tnibc->tnjic/dot_general | solution.py:58
  171.1 3.2 %fusion.213 = f32[2,20,20,20]{3,2,1,0:T(8,128)S(1)} fusion(f32[4,2,20,20,20]{4,3,2,1,0:T(8,128)S(1)} %fusion.212, f32[4,20,20,1,1]{2,1,0,3,4:T(8,128)S(1)} %reshape.229), kind=kOutput, calls=%fused_computation.2.clone.1 | convolution fusion | flops 15360000 | bytes 326400 | tf_op jit(solution)/shard_map/while/body/eval_jaxpr/tkc,tnjic->nijk/dot_general | solution.py:61
  179.3 4.8 %fusion.212 = f32[4,2,20,20,20]{4,3,2,1,0:T(8,128)S(1)} fusion(f32[4,2,20,20,20]{4,3,2,1,0:T(8,128)} %reshape.227, f32[4,20,20,1,1]{2,1,0,3,4:T(8,128)S(1)} %reshape.228), kind=kOutput, calls=%fused_computation.7.clone.1 | convolution fusion | flops 15360000 | bytes 518400 | tf_op jit(solution)/shard_map/while/body/eval_jaxpr/tjb,tnibc->tnjic/dot_general | solution.py:58
  184.1 3.2 %fusion.213 = f32[2,20,20,20]{3,2,1,0:T(8,128)S(1)} fusion(f32[4,2,20,20,20]{4,3,2,1,0:T(8,128)S(1)} %fusion.212, f32[4,20,20,1,1]{2,1,0,3,4:T(8,128)S(1)} %reshape.229), kind=kOutput, calls=%fused_computation.2.clone.1 | convolution fusion | flops 15360000 | bytes 326400 | tf_op jit(solution)/shard_map/while/body/eval_jaxpr/tkc,tnjic->nijk/dot_general | solution.py:61
  192.2 4.8 %fusion.212 = f32[4,2,20,20,20]{4,3,2,1,0:T(8,128)S(1)} fusion(f32[4,2,20,20,20]{4,3,2,1,0:T(8,128)} %reshape.227, f32[4,20,20,1,1]{2,1,0,3,4:T(8,128)S(1)} %reshape.228), kind=kOutput, calls=%fused_computation.7.clone.1 | convolution fusion | flops 15360000 | bytes 518400 | tf_op jit(solution)/shard_map/while/body/eval_jaxpr/tjb,tnibc->tnjic/dot_general | solution.py:58
  197.1 3.2 %fusion.213 = f32[2,20,20,20]{3,2,1,0:T(8,128)S(1)} fusion(f32[4,2,20,20,20]{4,3,2,1,0:T(8,128)S(1)} %fusion.212, f32[4,20,20,1,1]{2,1,0,3,4:T(8,128)S(1)} %reshape.229), kind=kOutput, calls=%fused_computation.2.clone.1 | convolution fusion | flops 15360000 | bytes 326400 | tf_op jit(solution)/shard_map/while/body/eval_jaxpr/tkc,tnjic->nijk/dot_general | solution.py:61
  205.2 4.8 %fusion.212 = f32[4,2,20,20,20]{4,3,2,1,0:T(8,128)S(1)} fusion(f32[4,2,20,20,20]{4,3,2,1,0:T(8,128)} %reshape.227, f32[4,20,20,1,1]{2,1,0,3,4:T(8,128)S(1)} %reshape.228), kind=kOutput, calls=%fused_computation.7.clone.1 | convolution fusion | flops 15360000 | bytes 518400 | tf_op jit(solution)/shard_map/while/body/eval_jaxpr/tjb,tnibc->tnjic/dot_general | solution.py:58
  218.2 4.8 %fusion.212 = f32[4,2,20,20,20]{4,3,2,1,0:T(8,128)S(1)} fusion(f32[4,2,20,20,20]{4,3,2,1,0:T(8,128)} %reshape.227, f32[4,20,20,1,1]{2,1,0,3,4:T(8,128)S(1)} %reshape.228), kind=kOutput, calls=%fused_computation.7.clone.1 | convolution fusion | flops 15360000 | bytes 518400 | tf_op jit(solution)/shard_map/while/body/eval_jaxpr/tjb,tnibc->tnjic/dot_general | solution.py:58
  223.1 3.2 %fusion.213 = f32[2,20,20,20]{3,2,1,0:T(8,128)S(1)} fusion(f32[4,2,20,20,20]{4,3,2,1,0:T(8,128)S(1)} %fusion.212, f32[4,20,20,1,1]{2,1,0,3,4:T(8,128)S(1)} %reshape.229), kind=kOutput, calls=%fused_computation.2.clone.1 | convolution fusion | flops 15360000 | bytes 326400 | tf_op jit(solution)/shard_map/while/body/eval_jaxpr/tkc,tnjic->nijk/dot_general | solution.py:61
  229.3 6.3 %all-to-all-start = ((f32[16,2,8000]{2,1,0:T(2,128)}), f32[16,2,8000]{2,1,0:T(2,128)S(1)}, u32[]{:S(2)}, u32[]{:S(2)}) async-start(f32[16,2,8000]{2,1,0:T(2,128)} %copy.43), calls=%async_computation | async-start | bytes 2064384 | tf_op jit(solution)/shard_map/all_to_all | solution.py:101
  243.8 18.3 %all-to-all-done = f32[16,2,8000]{2,1,0:T(2,128)S(1)} async-done(((f32[16,2,8000]{2,1,0:T(2,128)}), f32[16,2,8000]{2,1,0:T(2,128)S(1)}, u32[]{:S(2)}, u32[]{:S(2)}) %all-to-all-start) | async-done | bytes 1024032 | tf_op jit(solution)/shard_map/all_to_all | solution.py:101
  (243 shorter events, 123.2 us)
Async XLA Ops:
  0.0 30.1 %copy-start = (f32[20]{0:T(128)}, f32[20]{0:T(128)S(1)}, u32[]{:S(2)}) copy-start(f32[20]{0:T(128)S(1)} %add_multiply_fusion) | copy-start | bytes 244
  0.0 30.1 %copy-start.2 = (pred[20]{0:T(512)(128)(4,1)}, pred[20]{0:T(512)(128)(4,1)S(1)}, u32[]{:S(2)}) copy-start(pred[20]{0:T(512)(128)(4,1)S(1)} %broadcast_compare_fusion) | copy-start | bytes 64
  6.2 17.1 %copy-start.6 = (s32[1,8]{1,0:T(1,128)S(1)}, s32[1,8]{1,0:T(1,128)}, u32[]{:S(2)}) copy-start(s32[1,8]{1,0:T(1,128)} %param.19) | copy-start | bytes 100
  129.1 6.6 %copy-start.8 = (s32[7]{0:T(128)S(1)}, s32[7]{0:T(128)}, u32[]{:S(2)}) copy-start(s32[7]{0:T(128)} %get-tuple-element.200) | copy-start | bytes 88
  131.2 98.1 %all-to-all-start.1 = ((f32[8,2,8000]{2,1,0:T(2,128)}), f32[8,2,8000]{2,1,0:T(2,128)}, u32[]{:S(2)}, u32[]{:S(2)}) async-start(f32[8,2,8000]{2,1,0:T(2,128)} %copy.52), calls=%async_computation.1 | async-start | bytes 1032192 | tf_op jit(solution)/shard_map/all_to_all | solution.py:113
  135.7 90.9 %copy-start.5 = (s32[2,7,1]{1,2,0:T(1,128)S(1)}, s32[2,7,1]{1,2,0:T(1,128)}, u32[]{:S(2)}) copy-start(s32[2,7,1]{1,2,0:T(1,128)} %param.16) | copy-start | bytes 172
  135.7 90.9 %copy-start.4 = (s32[2,7]{1,0:T(2,128)S(1)}, s32[2,7]{1,0:T(2,128)}, u32[]{:S(2)}) copy-start(s32[2,7]{1,0:T(2,128)} %param.17) | copy-start | bytes 172
  227.8 7.8 %copy-start.7 = (s32[1,8]{1,0:T(1,128)S(1)}, s32[1,8]{1,0:T(1,128)}, u32[]{:S(2)}) copy-start(s32[1,8]{1,0:T(1,128)} %param.19) | copy-start | bytes 100
  229.3 7.9 %copy-start.1 = (f32[20]{0:T(128)S(1)}, f32[20]{0:T(128)}, u32[]{:S(2)}) copy-start(f32[20]{0:T(128)} %copy-done) | copy-start | bytes 244
  229.3 7.9 %copy-start.3 = (pred[20]{0:T(512)(128)(4,1)S(1)}, pred[20]{0:T(512)(128)(4,1)}, u32[]{:S(2)}) copy-start(pred[20]{0:T(512)(128)(4,1)} %copy-done.2) | copy-start | bytes 64
  229.3 32.8 %all-to-all-start = ((f32[16,2,8000]{2,1,0:T(2,128)}), f32[16,2,8000]{2,1,0:T(2,128)S(1)}, u32[]{:S(2)}, u32[]{:S(2)}) async-start(f32[16,2,8000]{2,1,0:T(2,128)} %copy.43), calls=%async_computation | async-start | bytes 2064384 | tf_op jit(solution)/shard_map/all_to_all | solution.py:101
where the time goes:
time: 279 us; the launch traced here: 274 us
  matrix products  138 us (49%)
  local copies, waits for them, and re-layouts  79.1 us (28%)
  waiting for transfers between devices  18.3 us (7%)
  blocking collectives  14.9 us (5%)
  other arithmetic  11 us (4%)
  starting transfers between devices  10.4 us (4%)
    dot_general x14, matrix products, per_disp(): jnp.einsum('tjb,tnibc->tnjic', second_factor, partial_value, precision=pr...  66.7 us
    dot_general x14, matrix products, per_disp(): jnp.einsum('tkc,tnjic->nijk', third_factor, partial_value, precision=prec...  45.1 us
    reshape x14, local copies, waits for them, and re-layouts, per_disp(): partial_value.reshape(term_count, node_count, edge_len, edge_len, edge_len)  27.4 us
    all_to_all x1, waiting for transfers between devices, on_device(): lax.all_to_all(middle_buffer, ('gy', 'gz'), split_axis=0, concat_axis=0,...  18.3 us
    all_gather x1, blocking collectives, on_device(): column = lax.all_gather(corner_parts, 'gz', axis=0, tiled=True)  14.9 us
    dot_general x12, matrix products, transform(): jnp.einsum('ix,jy,kz,nxyz->nijk', filter_table, filter_table, filter_tabl...  14.5 us
    dynamic_slice x14, local copies, waits for them, and re-layouts, contributions(): lax.scan(per_disp, jnp.zeros((), jnp.float32), (matrices, ranks, destinat...  13.1 us
    squeeze x14, local copies, waits for them, and re-layouts, contributions(): lax.scan(per_disp, jnp.zeros((), jnp.float32), (matrices, ranks, destinat...  10.4 us
  transfers between devices with their start and end apart: 2, of which 1 were waited for; matrix products, arithmetic and copies ran while one was open for 37% of the time, Pallas kernels for 0%

commit v1 on v0

v1 whole, which is shorter than its diff:
```python
import functools

import jax
import jax.numpy as jnp
from jax import lax
from jax.experimental import pallas as pl
from jax.experimental.pallas import tpu as pltpu
from jax.sharding import PartitionSpec as P

ORDER = 10
LANES = 128
CHUNK_ROWS = 72

precise = lax.Precision.HIGHEST


def two_scale(edge_len):
    row_index = jnp.arange(edge_len)[:, None].astype(jnp.float32)
    col_index = jnp.arange(edge_len)[None, :].astype(jnp.float32)
    filter_table = jnp.sqrt(2.0 / edge_len) * jnp.cos(
        jnp.pi * (col_index + 0.5) * row_index / edge_len
    )
    return jnp.where(row_index == 0, filter_table * jnp.sqrt(0.5), filter_table)


def transform(blocks, filter_table, inverse):
    if inverse:
        filter_table = filter_table.T
    return jnp.einsum(
        "ix,jy,kz,nxyz->nijk", filter_table, filter_table, filter_table, blocks, precision=precise
    )


def assemble(leaf_rows, order_len):
    node_count = leaf_rows.shape[0] // 8
    shaped = leaf_rows.reshape(node_count, 2, 2, 2, order_len, order_len, order_len)
    return shaped.transpose(0, 1, 4, 2, 5, 3, 6).reshape(
        node_count, 2 * order_len, 2 * order_len, 2 * order_len
    )


def split_octants(blocks, order_len):
    node_count = blocks.shape[0]
    shaped = blocks.reshape(node_count, 2, order_len, 2, order_len, 2, order_len)
    return shaped.transpose(0, 1, 3, 5, 2, 4, 6).reshape(node_count * 8, order_len**3)


def halves(value):
    high = value.astype(jnp.bfloat16)
    low = (value - high.astype(jnp.float32)).astype(jnp.bfloat16)
    return high, low


def nt_dot(a, b):
    return lax.dot_general(a, b, (((1,), (1,)), ((), ())), preferred_element_type=jnp.float32)


def tn_dot(a, b):
    return lax.dot_general(a, b, (((0,), (0,)), ((), ())), preferred_element_type=jnp.float32)


def images_kernel(
    edge, disp, nodes, padded, tiles,
    dest_ref, x_ref, third_ref, second_ref, first_ref, out_ref,
    ping_ref, pong_ref, coef_ref, image_ref,
):
    pairs = first_ref.shape[0]
    width = tiles * LANES
    rows = padded * edge
    spread = (
        lax.broadcasted_iota(jnp.int32, (pairs, width), 1) // edge
        == lax.broadcasted_iota(jnp.int32, (pairs, width), 0)
    ).astype(jnp.bfloat16)

    def fill(slot, source_ref):
        value = source_ref[...]
        high = value.astype(jnp.bfloat16)
        rest = value - high.astype(jnp.float32)
        mid, low = halves(rest)
        table = tn_dot(high, spread) + tn_dot(mid, spread) + tn_dot(low, spread)
        for tile in range(tiles):
            coef_ref[slot, tile] = table[:, tile * LANES:(tile + 1) * LANES]

    fill(0, second_ref)
    fill(1, first_ref)
    x_high, x_low = halves(x_ref[...])
    w_high, w_low = halves(third_ref[...])
    start = nt_dot(x_high, w_high) + (nt_dot(x_high, w_low) + nt_dot(x_low, w_high))
    for tile in range(tiles):
        ping_ref[tile] = start[:, tile * LANES:(tile + 1) * LANES]

    group = 4
    groups = edge // group

    def contract(slot, source_ref, target_ref):
        def step(index, carry):
            tile = index // groups
            first = (index % groups) * group
            sums = [jnp.zeros((rows, LANES), jnp.float32) for _ in range(group)]
            for b in range(edge):
                part = source_ref[tile, pl.ds(b, rows, stride=edge), :]
                for q in range(group):
                    factor = coef_ref[slot, tile, pl.ds((first + q) * edge + b, 1), :]
                    sums[q] = sums[q] + factor * part
            for q in range(group):
                at = pl.multiple_of((first + q) * rows, 8)
                target_ref[tile, pl.ds(at, rows), :] = sums[q]
            return carry

        lax.fori_loop(0, tiles * groups, step, 0)

    contract(0, ping_ref, pong_ref)
    contract(1, pong_ref, ping_ref)

    per_tile = LANES // edge
    columns = 2 * LANES
    lane = lax.broadcasted_iota(jnp.int32, (LANES, columns), 0)
    column = lax.broadcasted_iota(jnp.int32, (LANES, columns), 1)
    column_disp = (column // LANES) * per_tile + (column % LANES) // edge
    column_ok = (column % LANES) < per_tile * edge
    terms = pairs // disp
    total = None
    for tile in range(tiles):
        place = lane + tile * LANES
        pick = (
            (place // (edge * terms) == column_disp) & (place % edge == (column % LANES) % edge)
            & column_ok & (place < pairs * edge)
        ).astype(jnp.bfloat16)
        high, low = halves(ping_ref[tile])
        part = jnp.dot(high, pick, preferred_element_type=jnp.float32) + jnp.dot(
            low, pick, preferred_element_type=jnp.float32
        )
        total = part if total is None else total + part
    used = edge * edge * padded
    for half in range(2):
        image_ref[half, pl.ds(0, used), :] = total[:, half * LANES:(half + 1) * LANES]
        image_ref[half, pl.ds(used, image_ref.shape[1] - used), :] = jnp.zeros(
            (image_ref.shape[1] - used, LANES), jnp.float32
        )
    out_ref[...] = jnp.zeros_like(out_ref)
    out_lane = lax.broadcasted_iota(jnp.int32, (CHUNK_ROWS, LANES), 1) // edge
    for node in range(nodes):
        for e in range(disp):
            packed = jnp.zeros((CHUNK_ROWS, LANES), jnp.float32)
            for q in range(per_tile):
                chunk = image_ref[
                    e // per_tile, pl.ds(q * CHUNK_ROWS * padded + node, CHUNK_ROWS, stride=padded), :
                ]
                shift = (edge * (q - e % per_tile)) % LANES
                if shift:
                    chunk = pltpu.roll(chunk, shift, 1)
                packed = jnp.where(out_lane == q, chunk, packed)
            to = dest_ref[node, e]
            out_ref[to] = out_ref[to] + packed


def images(blocks, matrices, ranks, destination, buffer_rows):
    nodes, edge = blocks.shape[0], blocks.shape[1]
    disp, terms = matrices.shape[0], matrices.shape[1]
    pairs = disp * terms
    padded = nodes + nodes % 2
    tiles = -(-pairs * edge // LANES)
    flat = blocks.reshape(nodes * edge * edge, edge)
    flat = jnp.pad(flat, ((0, (padded - nodes) * edge * edge), (0, 0)))
    keep = (jnp.arange(terms, dtype=jnp.int32)[None, :] < ranks[:, None]).astype(jnp.float32)
    third = (matrices[:, :, 2] * keep[:, :, None]).reshape(pairs * edge, edge)
    third = jnp.pad(third, ((0, tiles * LANES - pairs * edge), (0, 0)))
    second = matrices[:, :, 1].reshape(pairs, edge * edge)
    first = matrices[:, :, 0].reshape(pairs, edge * edge)
    per_tile = LANES // edge
    vmem = pl.BlockSpec(memory_space=pltpu.VMEM)
    return pl.pallas_call(
        functools.partial(images_kernel, edge, disp, nodes, padded, tiles),
        out_shape=jax.ShapeDtypeStruct((buffer_rows, CHUNK_ROWS, LANES), jnp.float32),
        in_specs=[pl.BlockSpec(memory_space=pltpu.SMEM)] + [vmem] * 4,
        out_specs=vmem,
        scratch_shapes=[
            pltpu.VMEM((tiles, padded * edge * edge, LANES), jnp.float32),
            pltpu.VMEM((tiles, padded * edge * edge, LANES), jnp.float32),
            pltpu.VMEM((2, tiles, edge * edge, LANES), jnp.float32),
            pltpu.VMEM((2, padded * CHUNK_ROWS * per_tile, LANES), jnp.float32),
        ],
    )(destination, flat, third, second, first)


def unpack(rows, edge):
    per_tile = LANES // edge
    parts = rows[:, :, :per_tile * edge].reshape(-1, CHUNK_ROWS, per_tile, edge)
    parts = parts.transpose(0, 2, 1, 3).reshape(-1, per_tile * CHUNK_ROWS, edge)
    return parts[:, :edge * edge].reshape(-1, edge, edge, edge)


def on_device(
    leaf_coeffs, operator_blocks, term_ranks, target_device, target_slot, coarse_targets, parent_place
):
    edge_len = 2 * ORDER
    filter_table = two_scale(edge_len)
    node_count = leaf_coeffs.shape[0] // 8
    coarse_count = coarse_targets.shape[0]
    middle_blocks = transform(assemble(leaf_coeffs, ORDER), filter_table, False)
    count_gy = lax.axis_size("gy")
    count_gz = lax.axis_size("gz")
    corner_parts = middle_blocks[:, :ORDER, :ORDER, :ORDER].reshape(1, node_count, ORDER**3)
    column = lax.all_to_all(
        jnp.broadcast_to(corner_parts, (count_gz, node_count, ORDER**3)),
        "gz", split_axis=0, concat_axis=0, tiled=True,
    ).reshape(count_gz * node_count, ORDER**3)
    destination = target_device[:, :, 0] * node_count + target_slot
    middle_buffer = images(
        middle_blocks, operator_blocks[1], term_ranks[1], destination,
        count_gy * count_gz * node_count,
    )
    received = lax.all_to_all(middle_buffer, ("gy", "gz"), split_axis=0, concat_axis=0, tiled=True)
    slot_index = jnp.arange(coarse_count * 8, dtype=jnp.int32)[:, None]
    picker = (slot_index == parent_place[0][None, :]).astype(jnp.float32)
    octants = jnp.dot(picker, column, precision=precise, preferred_element_type=jnp.float32)
    coarse_blocks = transform(assemble(octants, ORDER), filter_table, False)
    buffer_rows = lax.axis_size("gx") * lax.axis_size("gy") * coarse_count
    coarse_buffer = images(
        coarse_blocks, operator_blocks[0], term_ranks[0], coarse_targets, buffer_rows
    )
    arrived = lax.all_to_all(coarse_buffer, ("gx", "gy"), split_axis=0, concat_axis=0, tiled=True)
    coarse_applied = unpack(
        jnp.sum(arrived.reshape(-1, coarse_count, CHUNK_ROWS, LANES), axis=0), edge_len
    )
    coarse_back = split_octants(transform(coarse_applied, filter_table, True), ORDER)
    own_picker = lax.dynamic_slice_in_dim(picker, lax.axis_index("gz") * node_count, node_count, 1)
    from_parent = jnp.dot(
        own_picker.T, coarse_back, precision=precise, preferred_element_type=jnp.float32
    )
    middle_total = unpack(
        jnp.sum(received.reshape(-1, node_count, CHUNK_ROWS, LANES), axis=0), edge_len
    )
    middle_total = middle_total.at[:, :ORDER, :ORDER, :ORDER].add(
        from_parent.reshape(node_count, ORDER, ORDER, ORDER)
    )
    return split_octants(transform(middle_total, filter_table, True), ORDER)


def solution(mesh):
    in_specs = (
        P(("gx", "gy", "gz"), None),
        P(),
        P(),
        P(("gx", "gy", "gz"), None, None),
        P(("gx", "gy", "gz"), None),
        P(("gx", "gy"), None),
        P(("gx", "gy"), None),
    )
    out_specs = P(("gx", "gy", "gz"), None)
    return jax.shard_map(
        on_device, mesh=mesh, in_specs=in_specs, out_specs=out_specs, check_vma=False
    )
```

time: 279 us -> 107 us (0.38); the launches traced: 274 us -> 107 us
  matrix products: 138 us -> 18.6 us
  local copies, waits for them, and re-layouts: 79.1 us -> 20.9 us
  Pallas kernels: 0 us -> 26.8 us
  blocking collectives: 14.9 us -> 0 us
  other arithmetic: 11 us -> 0.93 us
  waiting for transfers between devices: 18.3 us -> 25.3 us
  starting transfers between devices: 10.4 us -> 13.8 us
    dot_general x44 -> x0, matrix products: 121 us -> none  [the longest x14 66.7 us: per_disp(): jnp.einsum('tjb,tnibc->tnjic', second_factor, partial_value, precision=pr...]
    pallas_call x0 -> x2, Pallas kernels: none -> 26.8 us  [images(): pl.pallas_call(functools.partial(images_kernel, edge, disp, nodes, padded...]
    reshape x20 -> x7, local copies, waits for them, and re-layouts: 29 us -> 2.46 us  [the longest x2 1.58 us: images(): flat = blocks.reshape(nodes * edge * edge, edge)]
    squeeze x57 -> x2, local copies, waits for them, and re-layouts: 15.5 us -> 0.34 us  [images(): third = (matrices[:, :, 2] * keep[:, :, None]).reshape(pairs * edge, edge)]
    all_gather x1 -> x0, blocking collectives: 14.9 us -> none  [on_device(): column = lax.all_gather(corner_parts, 'gz', axis=0, tiled=True)]
    dynamic_slice x14 -> x0, local copies, waits for them, and re-layouts: 13.1 us -> none  [contributions(): lax.scan(per_disp, jnp.zeros((), jnp.float32), (matrices, ranks, destinat...]
    convert_element_type x14 -> x1, other arithmetic: 8.75 us -> 0.07 us  [images(): (jnp.arange(terms, dtype=jnp.int32)[None, :] < ranks[:, None]).astype(jnp...]
    all_to_all x0 -> x1, starting transfers between devices: none -> 6.35 us  [on_device(): lax.all_to_all(jnp.broadcast_to(corner_parts, (count_gz, node_count, ORDE...]
  transfers between devices with their start and end apart: 2 -> 3, of which waited for: 1 -> 2; matrix products, arithmetic and copies ran while one was open for 37% -> 13% of each run, Pallas kernels for 0% -> 13%
where the time goes in v1:
time: 107 us
  Pallas kernels  26.8 us (25%)
  waiting for transfers between devices  25.3 us (24%)
  local copies, waits for them, and re-layouts  20.9 us (20%)
  matrix products  18.6 us (17%)
  starting transfers between devices  13.8 us (13%)
    pallas_call x2, Pallas kernels, images(): pl.pallas_call(functools.partial(images_kernel, edge, disp, nodes, padded...  26.8 us
    all_to_all x1, waiting for transfers between devices, on_device(): lax.all_to_all(middle_buffer, ('gy', 'gz'), split_axis=0, concat_axis=0,...  22.3 us
    dot_general x12, matrix products, transform(): jnp.einsum('ix,jy,kz,nxyz->nijk', filter_table, filter_table, filter_tabl...  14.5 us
    all_to_all x1, starting transfers between devices, on_device(): lax.all_to_all(jnp.broadcast_to(corner_parts, (count_gz, node_count, ORDE...  6.35 us
    reshape x4, local copies, waits for them, and re-layouts, assemble(): shaped.transpose(0, 1, 4, 2, 5, 3, 6)  3.83 us
    all_to_all x1, starting transfers between devices, on_device(): lax.all_to_all(coarse_buffer, ('gx', 'gy'), split_axis=0, concat_axis=0,...  3.76 us
    all_to_all x1, starting transfers between devices, on_device(): lax.all_to_all(middle_buffer, ('gy', 'gz'), split_axis=0, concat_axis=0,...  3.7 us
    dot_general x1, matrix products, on_device(): jnp.dot(own_picker.T, coarse_back, precision=precise, preferred_element_t...  2.96 us
  transfers between devices with their start and end apart: 3, of which 2 were waited for; matrix products, arithmetic and copies ran while one was open for 13% of the time, Pallas kernels for 13%

profile of v1, /device:TPU:0, one launch (start us, length us, event | category | flops | bytes accessed | tf_op | source)
XLA Modules:
  0.0 106.7 jit_solution(3786762607227770203)
XLA Ops:
  0.0 1.4 %reshape.203 = f32[2,2,2,2,10,10,10]{6,5,4,3,2,1,0:T(8,128)S(1)} reshape(f32[16,1000]{1,0:T(8,128)} %param.9) | data formatting | bytes 128000 | tf_op jit(solution)/shard_map/reshape | solution.py:36
  2.5 0.7 convolution_bitcast_fusion.1
  3.2 0.7 fusion.4
  3.9 0.7 fusion.25
  5.3 6.4 %all-to-all-start.1 = ((f32[4,2,1000]{2,1,0:T(2,128)}), f32[4,2,1000]{2,1,0:T(2,128)S(1)}, u32[]{:S(2)}, u32[]{:S(2)}) async-start(f32[4,2,1000]{2,1,0:T(2,128)} %broadcast_in_dim.46), calls=%async_computation.1 | async-start | bytes 65536 | tf_op jit(solution)/shard_map/all_to_all | solution.py:204
  12.3 0.7 reshape_squeeze.14.second_ref
  13.6 0.8 pad.12.third_ref
  14.4 3.0 %all-to-all-done.1 = f32[4,2,1000]{2,1,0:T(2,128)S(1)} async-done(((f32[4,2,1000]{2,1,0:T(2,128)}), f32[4,2,1000]{2,1,0:T(2,128)S(1)}, u32[]{:S(2)}, u32[]{:S(2)}) %all-to-all-start.1) | async-done | bytes 32032 | tf_op jit(solution)/shard_map/all_to_all | solution.py:204
  17.6 1.2 %convolution_bitcast_fusion = f32[2,2,10,2,10,2,10]{6,5,4,2,3,1,0:T(2,128)S(1)} fusion(f32[10,10,10,8,1,1,1]{2,1,0,3,6,5,4:T(8,128)S(1)} %bitcast.114, s32[8]{0:T(128)S(1)} %bitcast.124, s32[2,2,2,2]{3,2,1,0:T(2,128)S(1)} %multiply_add_fusion), kind=kOutput, calls=%fused_computation | convolution fusion | flops 1536128 | bytes 96096 | tf_op jit(solution)/shard_map/dot_general | solution.py:216
  18.8 2.2 %copy.69 = f32[2,2,10,2,10,2,10]{2,1,6,5,4,3,0:T(2,128)S(1)} copy(f32[2,2,10,2,10,2,10]{6,5,4,2,3,1,0:T(2,128)S(1)} %convolution_bitcast_fusion) | data formatting | bytes 128000 | tf_op jit(solution)/shard_map/reshape | solution.py:37
  21.5 0.7 fusion.23
  22.5 2.6 %fusion.21 = f32[2,20,20,20]{1,3,2,0:T(8,128)S(1)} fusion(f32[2,20,20,20]{1,2,3,0:T(8,128)S(1)} %copy.35, f32[20]{0:T(128)S(1)} %iota_convert_fusion, f32[20]{0:T(128)S(1)} %add_multiply_fusion, pred[20]{0:T(512)(128)(4,1)S(1)} %broadcast_compare_fusion), kind=kOutput, calls=%fused_computation.26 | convolution fusion | flops 3842000 | bytes 128180 | tf_op jit(solution)/shard_map/ix,jy,kz,nxyz->nijk/dot_general | solution.py:29
  25.2 0.7 fusion.19
  25.8 0.8 reshape.228.x_ref
  26.6 13.3 %shard_map.74 = f32[16,72,128]{2,1,0:T(8,128)} custom-call(s32[2,7]{1,0:T(2,128)} %dest_ref.1, f32[800,20]{1,0:T(8,128)} %reshape.228.x_ref, f32[640,20]{1,0:T(8,128)} %pad.12.third_ref, f32[28,400]{1,0:T(8,128)} %reshape_squeeze.14.second_ref, f32[28,400]{1,0:T(8,128)} %reshape_squeeze.15.first_ref), custom_call_target="tpu_custom_call" | custom-call | tf_op jit(solution)/shard_map/pallas_call | solution.py:172
  39.9 3.8 %all-to-all-start.2 = ((f32[16,72,128]{2,1,0:T(8,128)}), f32[16,72,128]{2,1,0:T(8,128)S(1)}, u32[]{:S(2)}, u32[]{:S(2)}) async-start(f32[16,72,128]{2,1,0:T(8,128)} %shard_map.74), calls=%async_computation.2 | async-start | bytes 1179648 | tf_op jit(solution)/shard_map/all_to_all | solution.py:222
  43.7 0.8 reshape.226.x_ref
  44.9 0.7 pad.11.third_ref
  47.6 13.5 %shard_map.73 = f32[32,72,128]{2,1,0:T(8,128)} custom-call(s32[2,7]{1,0:T(2,128)} %add.59.dest_ref, f32[800,20]{1,0:T(8,128)} %reshape.226.x_ref, f32[640,20]{1,0:T(8,128)} %pad.11.third_ref, f32[28,400]{1,0:T(8,128)} %reshape_squeeze.12.second_ref, f32[28,400]{1,0:T(8,128)} %reshape_squeeze.13.first_ref), custom_call_target="tpu_custom_call" | custom-call | tf_op jit(solution)/shard_map/pallas_call | solution.py:172
  61.1 3.7 %all-to-all-start = ((f32[32,72,128]{2,1,0:T(8,128)}), f32[32,72,128]{2,1,0:T(8,128)S(1)}, u32[]{:S(2)}, u32[]{:S(2)}) async-start(f32[32,72,128]{2,1,0:T(8,128)} %shard_map.73), calls=%async_computation | async-start | bytes 2359296 | tf_op jit(solution)/shard_map/all_to_all | solution.py:213
  65.5 1.0 fusion.2
  66.9 2.7 %fusion.16 = f32[2,20,20,20]{1,3,2,0:T(8,128)S(1)} fusion(f32[2,20,20,20]{1,2,3,0:T(8,128)S(1)} %copy.42, f32[20]{0:T(128)S(1)} %iota_convert_fusion, f32[20]{0:T(128)S(1)} %add_multiply_fusion, pred[20]{0:T(512)(128)(4,1)S(1)} %broadcast_compare_fusion), kind=kOutput, calls=%fused_computation.21 | convolution fusion | flops 3842000 | bytes 128180 | tf_op jit(solution)/shard_map/ix,jy,kz,nxyz->nijk/dot_general | solution.py:29
  69.6 0.6 fusion.14
  70.5 0.7 reshape.217
  72.1 22.3 %all-to-all-done = f32[32,72,128]{2,1,0:T(8,128)S(1)} async-done(((f32[32,72,128]{2,1,0:T(8,128)}), f32[32,72,128]{2,1,0:T(8,128)S(1)}, u32[]{:S(2)}, u32[]{:S(2)}) %all-to-all-start) | async-done | bytes 1179680 | tf_op jit(solution)/shard_map/all_to_all | solution.py:213
  95.3 3.0 %convolution_add_fusion = f32[2,10,10,10]{3,0,2,1:T(2,128)S(1)} fusion(f32[2,10,10,10]{3,0,2,1:T(2,128)S(1)} %copy.77, f32[10,10,10,16]{3,2,1,0:T(8,128)S(1)} %dot_general.66, pred[16,8]{0,1:T(8,128)(4,1)S(1)} %iota_compare_fusion.1, s32[]{:T(128)S(6)} %select_n.30), kind=kOutput, calls=%fused_computation.2 | convolution fusion | flops 386000 | bytes 930116 | tf_op jit(solution)/shard_map/dot_general | solution.py:228
  98.6 1.1 %scatter-add.4 = f32[2,20,20,20]{2,1,0,3:T(8,128)S(1)} dynamic-update-slice(f32[2,20,20,20]{2,1,0,3:T(8,128)S(1)} %reshape.209, f32[2,10,10,10]{2,1,0,3:T(8,128)S(1)} %copy.47, s32[]{:T(128)} %constant.57.clone.1, s32[]{:T(128)} %constant.57.clone.1, s32[]{:T(128)} %constant.57.clone.1, s32[]{:T(128)} %constant.57.clone.1) | dynamic-update-slice | bytes 16004 | tf_op jit(solution)/shard_map/scatter-add | solution.py:234
  99.7 1.0 fusion
  101.1 2.7 %fusion.11 = f32[2,20,20,20]{1,3,2,0:T(8,128)S(1)} fusion(f32[2,20,20,20]{1,2,3,0:T(8,128)S(1)} %copy.49, f32[20]{0:T(128)S(1)} %iota_convert_fusion, f32[20]{0:T(128)S(1)} %add_multiply_fusion, pred[20]{0:T(512)(128)(4,1)S(1)} %broadcast_compare_fusion), kind=kOutput, calls=%fused_computation.16 | convolution fusion | flops 3842000 | bytes 128180 | tf_op jit(solution)/shard_map/ix,jy,kz,nxyz->nijk/dot_general | solution.py:29
  103.8 0.7 fusion.9
  104.8 0.7 reshape.219
  105.7 1.0 reshape.220
  (64 shorter events, 10.9 us)
Async XLA Ops:
  3.2 8.5 %copy-start = (f32[2,7,4,3,400]{4,2,3,1,0:T(4,128)S(1)}, f32[2,7,4,3,400]{4,2,3,1,0:T(4,128)}, u32[]{:S(2)}) copy-start(f32[2,7,4,3,400]{4,2,3,1,0:T(4,128)} %param.10) | copy-start | bytes 806404
  3.8 7.8 %copy-start.2 = (s32[2,7]{1,0:T(2,128)S(1)}, s32[2,7]{1,0:T(2,128)}, u32[]{:S(2)}) copy-start(s32[2,7]{1,0:T(2,128)} %param.11) | copy-start | bytes 172
  5.3 12.0 %all-to-all-start.1 = ((f32[4,2,1000]{2,1,0:T(2,128)}), f32[4,2,1000]{2,1,0:T(2,128)S(1)}, u32[]{:S(2)}, u32[]{:S(2)}) async-start(f32[4,2,1000]{2,1,0:T(2,128)} %broadcast_in_dim.46), calls=%async_computation.1 | async-start | bytes 65536 | tf_op jit(solution)/shard_map/all_to_all | solution.py:204
  12.3 5.3 %copy-start.4 = (s32[1,8]{1,0:T(1,128)S(1)}, s32[1,8]{1,0:T(1,128)}, u32[]{:S(2)}) copy-start(s32[1,8]{1,0:T(1,128)} %param.15) | copy-start | bytes 100
  39.9 21.2 %all-to-all-start.2 = ((f32[16,72,128]{2,1,0:T(8,128)}), f32[16,72,128]{2,1,0:T(8,128)S(1)}, u32[]{:S(2)}, u32[]{:S(2)}) async-start(f32[16,72,128]{2,1,0:T(8,128)} %shard_map.74), calls=%async_computation.2 | async-start | bytes 1179648 | tf_op jit(solution)/shard_map/all_to_all | solution.py:222
  44.5 2.5 %copy-start.3 = (s32[2,7,1]{1,2,0:T(1,128)S(1)}, s32[2,7,1]{1,2,0:T(1,128)}, u32[]{:S(2)}) copy-start(s32[2,7,1]{1,2,0:T(1,128)} %param.12) | copy-start | bytes 172
  44.5 2.5 %copy-start.1 = (s32[2,7]{1,0:T(2,128)S(1)}, s32[2,7]{1,0:T(2,128)}, u32[]{:S(2)}) copy-start(s32[2,7]{1,0:T(2,128)} %param.13) | copy-start | bytes 172
  61.1 33.3 %all-to-all-start = ((f32[32,72,128]{2,1,0:T(8,128)}), f32[32,72,128]{2,1,0:T(8,128)S(1)}, u32[]{:S(2)}, u32[]{:S(2)}) async-start(f32[32,72,128]{2,1,0:T(8,128)} %shard_map.73), calls=%async_computation | async-start | bytes 2359296 | tf_op jit(solution)/shard_map/all_to_all | solution.py:213

commit v2 on v1

v2 whole, which is shorter than its diff:
```python
import functools

import jax
import jax.numpy as jnp
import numpy as np
from jax import lax
from jax.experimental import pallas as pl
from jax.experimental.pallas import tpu as pltpu
from jax.sharding import PartitionSpec as P

ORDER = 10
LANES = 128
CHUNK_ROWS = 72

def ceil_to(value, step):
    return -(-value // step) * step


@functools.cache
def tables(order):
    edge = 2 * order
    i, x = np.arange(edge)[:, None], np.arange(edge)[None, :]
    h = np.sqrt(2.0 / edge) * np.cos(np.pi * (x + 0.5) * i / edge) * np.where(i == 0, np.sqrt(0.5), 1.0)
    face = order * order
    block = ceil_to(face, 8)
    cells = edge * edge
    per_tile = LANES // edge
    square = np.zeros((cells, 4, block))
    whole = np.einsum("ixa,jyb->ijxyab", h.reshape(edge, 2, order), h.reshape(edge, 2, order))
    square[:, :, :face] = whole.reshape(cells, 4, face)
    square = square.reshape(cells, 4 * block)
    low = square.reshape(edge, edge, -1)[:order, :order].reshape(face, -1)
    corner = np.zeros((LANES, 4 * block))
    corner[:face] = low
    forward = np.concatenate([square, corner])
    inverse = np.zeros((4 * block, per_tile * CHUNK_ROWS))
    inverse[:, :cells] = square.T
    inner = np.zeros((4 * block, block))
    inner[:, :face] = low.T
    pad = ceil_to(order, 8)
    lane_place = np.zeros((2, pad, edge))
    lane_back = np.zeros((2, edge, edge))
    for o in range(2):
        lane_place[o, :order] = h.T[o * order:(o + 1) * order]
        lane_back[o, o * order:(o + 1) * order] = h[:order]
    lane_inverse = np.zeros((LANES, edge))
    lane_inverse[:edge] = h
    head = np.zeros((pad, edge))
    head[:] = h[:pad]

    def split(value):
        high = value.astype(np.float32).astype(jnp.bfloat16)
        return np.stack([high, (value - high.astype(np.float64)).astype(np.float32).astype(jnp.bfloat16)])

    plain = lambda value: value.astype(np.float32)
    return dict(
        forward=split(forward), inverse=split(inverse), inner=split(inner),
        h=plain(h), head=plain(head), lane_place=plain(lane_place), lane_back=plain(lane_back),
        lane_inverse=plain(lane_inverse),
    )


def table_dot(table_ref, value, rows=None):
    high, low = halves(value)
    dot = lambda a, b: jnp.dot(a, b, preferred_element_type=jnp.float32)
    first, second = table_ref[0, :rows], table_ref[1, :rows]
    return dot(first, high) + (dot(first, low) + dot(second, high))


def split_dot(dot, a, b):
    a_high, a_low = halves(a)
    b_high, b_low = halves(b)
    return dot(a_high, b_high) + (dot(a_high, b_low) + dot(a_low, b_high))


def nn_dot(a, b):
    return jnp.dot(a, b, preferred_element_type=jnp.float32)


def halves(value):
    high = value.astype(jnp.bfloat16)
    low = (value - high.astype(jnp.float32)).astype(jnp.bfloat16)
    return high, low


def nt_dot(a, b):
    return lax.dot_general(a, b, (((1,), (1,)), ((), ())), preferred_element_type=jnp.float32)


def tn_dot(a, b):
    return lax.dot_general(a, b, (((0,), (0,)), ((), ())), preferred_element_type=jnp.float32)


def images_body(
    edge, disp, nodes, padded, tiles, block_of,
    dest_ref, third_ref, second_ref, first_ref, out_ref,
    ping_ref, pong_ref, coef_ref, image_ref,
):
    pairs = first_ref.shape[0]
    width = tiles * LANES
    rows = padded * edge
    spread = (
        lax.broadcasted_iota(jnp.int32, (pairs, width), 1) // edge
        == lax.broadcasted_iota(jnp.int32, (pairs, width), 0)
    ).astype(jnp.bfloat16)

    def fill(slot, source_ref):
        value = source_ref[...]
        high = value.astype(jnp.bfloat16)
        rest = value - high.astype(jnp.float32)
        mid, low = halves(rest)
        table = tn_dot(high, spread) + tn_dot(mid, spread) + tn_dot(low, spread)
        for tile in range(tiles):
            coef_ref[slot, tile] = table[:, tile * LANES:(tile + 1) * LANES]

    fill(0, second_ref)
    fill(1, first_ref)
    w_high, w_low = halves(third_ref[...])
    cells = edge * edge
    for node in range(padded):
        at = slice(node * cells, (node + 1) * cells)
        if node < nodes:
            x_high, x_low = halves(block_of(node))
            start = nt_dot(x_high, w_high) + (nt_dot(x_high, w_low) + nt_dot(x_low, w_high))
        for tile in range(tiles):
            if node < nodes:
                ping_ref[tile, at, :] = start[:, tile * LANES:(tile + 1) * LANES]
            else:
                ping_ref[tile, at, :] = jnp.zeros((cells, LANES), jnp.float32)

    group = 4
    groups = edge // group

    def contract(slot, source_ref, target_ref):
        def step(index, carry):
            tile = index // groups
            first = (index % groups) * group
            sums = [jnp.zeros((rows, LANES), jnp.float32) for _ in range(group)]
            for b in range(edge):
                part = source_ref[tile, pl.ds(b, rows, stride=edge), :]
                for q in range(group):
                    factor = coef_ref[slot, tile, pl.ds((first + q) * edge + b, 1), :]
                    sums[q] = sums[q] + factor * part
            for q in range(group):
                at = pl.multiple_of((first + q) * rows, 8)
                target_ref[tile, pl.ds(at, rows), :] = sums[q]
            return carry

        lax.fori_loop(0, tiles * groups, step, 0)

    contract(0, ping_ref, pong_ref)
    contract(1, pong_ref, ping_ref)

    per_tile = LANES // edge
    columns = 2 * LANES
    lane = lax.broadcasted_iota(jnp.int32, (LANES, columns), 0)
    column = lax.broadcasted_iota(jnp.int32, (LANES, columns), 1)
    column_disp = (column // LANES) * per_tile + (column % LANES) // edge
    column_ok = (column % LANES) < per_tile * edge
    terms = pairs // disp
    total = None
    for tile in range(tiles):
        place = lane + tile * LANES
        pick = (
            (place // (edge * terms) == column_disp) & (place % edge == (column % LANES) % edge)
            & column_ok & (place < pairs * edge)
        ).astype(jnp.bfloat16)
        high, low = halves(ping_ref[tile])
        part = jnp.dot(high, pick, preferred_element_type=jnp.float32) + jnp.dot(
            low, pick, preferred_element_type=jnp.float32
        )
        total = part if total is None else total + part
    used = edge * edge * padded
    for half in range(2):
        image_ref[half, pl.ds(0, used), :] = total[:, half * LANES:(half + 1) * LANES]
        image_ref[half, pl.ds(used, image_ref.shape[1] - used), :] = jnp.zeros(
            (image_ref.shape[1] - used, LANES), jnp.float32
        )
    out_ref[...] = jnp.zeros_like(out_ref)
    out_lane = lax.broadcasted_iota(jnp.int32, (CHUNK_ROWS, LANES), 1) // edge
    for node in range(nodes):
        for e in range(disp):
            packed = jnp.zeros((CHUNK_ROWS, LANES), jnp.float32)
            for q in range(per_tile):
                chunk = image_ref[
                    e // per_tile, pl.ds(q * CHUNK_ROWS * padded + node, CHUNK_ROWS, stride=padded), :
                ]
                shift = (edge * (q - e % per_tile)) % LANES
                if shift:
                    chunk = pltpu.roll(chunk, shift, 1)
                packed = jnp.where(out_lane == q, chunk, packed)
            to = dest_ref[node, e]
            out_ref[to] = out_ref[to] + packed


def middle_images_kernel(sizes, dest_ref, x_ref, third_ref, second_ref, first_ref, *rest):
    images_body(*sizes, lambda node: x_ref[node], dest_ref, third_ref, second_ref, first_ref, *rest)


def coarse_images_kernel(
    sizes, dest_ref, place_ref, column_ref, square_ref, lane_ref,
    third_ref, second_ref, first_ref, *rest,
):
    members = column_ref.shape[0]
    block = square_ref.shape[2] // 4
    spread = []
    for g in range(members):
        table = jnp.where(place_ref[0, g] % 2 == 0, lane_ref[0], lane_ref[1])
        spread.append(split_dot(tn_dot, column_ref[g], table)[:block])

    def block_of(node):
        parts = []
        for quarter in range(4):
            part = jnp.zeros((block, spread[0].shape[1]), jnp.float32)
            for g in range(members):
                here = place_ref[0, g] // 2 == node * 4 + quarter
                part = part + jnp.where(here, spread[g], 0.0)
            parts.append(part)
        return table_dot(square_ref, jnp.concatenate(parts, axis=0), spread[0].shape[1] ** 2)

    images_body(*sizes, block_of, dest_ref, third_ref, second_ref, first_ref, *rest)


VMEM = pl.BlockSpec(memory_space=pltpu.VMEM)
SMEM = pl.BlockSpec(memory_space=pltpu.SMEM)


def images(kernel, nodes, edge, scalars, extra, matrices, ranks, buffer_rows):
    disp, terms = matrices.shape[0], matrices.shape[1]
    pairs = disp * terms
    padded = nodes + nodes % 2
    tiles = -(-pairs * edge // LANES)
    keep = (jnp.arange(terms, dtype=jnp.int32)[None, :] < ranks[:, None]).astype(jnp.float32)
    third = (matrices[:, :, 2] * keep[:, :, None]).reshape(pairs * edge, edge)
    third = jnp.pad(third, ((0, tiles * LANES - pairs * edge), (0, 0)))
    second = matrices[:, :, 1].reshape(pairs, edge * edge)
    first = matrices[:, :, 0].reshape(pairs, edge * edge)
    per_tile = LANES // edge
    return pl.pallas_call(
        functools.partial(kernel, (edge, disp, nodes, padded, tiles)),
        out_shape=jax.ShapeDtypeStruct((buffer_rows, CHUNK_ROWS, LANES), jnp.float32),
        in_specs=[SMEM] * len(scalars) + [VMEM] * (len(extra) + 3),
        out_specs=VMEM,
        scratch_shapes=[
            pltpu.VMEM((tiles, padded * edge * edge, LANES), jnp.float32),
            pltpu.VMEM((tiles, padded * edge * edge, LANES), jnp.float32),
            pltpu.VMEM((2, tiles, edge * edge, LANES), jnp.float32),
            pltpu.VMEM((2, padded * CHUNK_ROWS * per_tile, LANES), jnp.float32),
        ],
    )(*scalars, *extra, third, second, first)


def forward_kernel(leaf_ref, forward_ref, h_ref, head_ref, x_ref, corner_ref):
    cells = x_ref.shape[1]
    for node in range(x_ref.shape[0]):
        rows = table_dot(forward_ref, leaf_ref[node])
        x_ref[node] = split_dot(nt_dot, rows[:cells], h_ref[...])
        corner_ref[node] = split_dot(nt_dot, head_ref[...], rows[cells:])


def unpacked(packed, edge, scratch_ref):
    for q in range(LANES // edge):
        chunk = pltpu.roll(packed, (LANES - edge * q) % LANES, 1) if q else packed
        scratch_ref[q * CHUNK_ROWS:(q + 1) * CHUNK_ROWS, :] = chunk
    return scratch_ref[...]


def back_kernel(place_ref, arrived_ref, inverse_ref, lane_inverse_ref, lane_back_ref, out_ref, scratch_ref):
    sources, coarse = arrived_ref.shape[:2]
    edge = out_ref.shape[2]
    block = out_ref.shape[1]
    backs = []
    for p in range(coarse):
        total = arrived_ref[0, p]
        for source in range(1, sources):
            total = total + arrived_ref[source, p]
        lanes = split_dot(nn_dot, unpacked(total, edge, scratch_ref), lane_inverse_ref[...])
        backs.append(table_dot(inverse_ref, lanes))
    for node in range(out_ref.shape[0]):
        place = place_ref[0, node]
        part = jnp.zeros((block, edge), jnp.float32)
        for p in range(coarse):
            for quarter in range(4):
                here = place // 2 == p * 4 + quarter
                part = part + jnp.where(here, backs[p][quarter * block:(quarter + 1) * block], 0.0)
        table = jnp.where(place % 2 == 0, lane_back_ref[0], lane_back_ref[1])
        out_ref[node] = split_dot(nn_dot, part, table)


def final_kernel(received_ref, parent_ref, inverse_ref, inner_ref, lane_inverse_ref, out_ref, scratch_ref):
    sources, nodes = received_ref.shape[:2]
    edge = out_ref.shape[2]
    for node in range(nodes):
        total = received_ref[0, node]
        for source in range(1, sources):
            total = total + received_ref[source, node]
        lanes = split_dot(nn_dot, unpacked(total, edge, scratch_ref), lane_inverse_ref[...])
        out_ref[node] = table_dot(inverse_ref, lanes) + table_dot(inner_ref, parent_ref[node])


def on_device(
    leaf_coeffs, operator_blocks, term_ranks, target_device, target_slot, coarse_targets, parent_place
):
    order = ORDER
    edge = 2 * order
    face, cells = order * order, edge * edge
    block = ceil_to(face, 8)
    table = tables(order)
    nodes = leaf_coeffs.shape[0] // 8
    coarse = coarse_targets.shape[0]
    count_gx, count_gy, count_gz = (lax.axis_size(name) for name in ("gx", "gy", "gz"))
    pad = table["head"].shape[0]
    scratch = [pltpu.VMEM((LANES // edge * CHUNK_ROWS, LANES), jnp.float32)]

    leaves = leaf_coeffs.reshape(nodes, 4, 2, face, order).transpose(0, 1, 3, 2, 4)
    leaves = jnp.pad(leaves.reshape(nodes, 4, face, edge), ((0, 0), (0, 0), (0, block - face), (0, 0)))
    middle, corners = pl.pallas_call(
        forward_kernel,
        out_shape=(
            jax.ShapeDtypeStruct((nodes, cells, edge), jnp.float32),
            jax.ShapeDtypeStruct((nodes, pad, LANES), jnp.float32),
        ),
        in_specs=[VMEM] * 4,
        out_specs=(VMEM, VMEM),
    )(leaves.reshape(nodes, 4 * block, edge), table["forward"], table["h"], table["head"])
    column = lax.all_to_all(
        jnp.broadcast_to(corners[None], (count_gz,) + corners.shape).reshape(-1, pad, LANES),
        "gz", split_axis=0, concat_axis=0, tiled=True,
    )
    destination = target_device[:, :, 0] * nodes + target_slot
    middle_buffer = images(
        middle_images_kernel, nodes, edge, (destination,), (middle,),
        operator_blocks[1], term_ranks[1], count_gy * count_gz * nodes,
    )
    middle_buffer, column = lax.optimization_barrier((middle_buffer, column))
    received = lax.all_to_all(middle_buffer, ("gy", "gz"), split_axis=0, concat_axis=0, tiled=True)
    coarse_buffer = images(
        coarse_images_kernel, coarse, edge, (coarse_targets, parent_place),
        (column, table["forward"], table["lane_place"]),
        operator_blocks[0], term_ranks[0], count_gx * count_gy * coarse,
    )
    arrived = lax.all_to_all(coarse_buffer, ("gx", "gy"), split_axis=0, concat_axis=0, tiled=True)
    own_place = lax.dynamic_slice_in_dim(parent_place, lax.axis_index("gz") * nodes, nodes, 1)
    parent = pl.pallas_call(
        back_kernel,
        out_shape=jax.ShapeDtypeStruct((nodes, block, edge), jnp.float32),
        in_specs=[SMEM] + [VMEM] * 4,
        out_specs=VMEM,
        scratch_shapes=scratch,
    )(
        own_place, arrived.reshape(-1, coarse, CHUNK_ROWS, LANES), table["inverse"],
        table["lane_inverse"], table["lane_back"],
    )
    result = pl.pallas_call(
        final_kernel,
        out_shape=jax.ShapeDtypeStruct((nodes, 4 * block, edge), jnp.float32),
        in_specs=[VMEM] * 5,
        out_specs=VMEM,
        scratch_shapes=scratch,
    )(
        received.reshape(-1, nodes, CHUNK_ROWS, LANES), parent, table["inverse"], table["inner"],
        table["lane_inverse"],
    )
    result = result.reshape(nodes, 4, block, 2, order)[:, :, :face]
    return result.transpose(0, 1, 3, 2, 4).reshape(nodes * 8, face * order)


def solution(mesh):
    in_specs = (
        P(("gx", "gy", "gz"), None),
        P(),
        P(),
        P(("gx", "gy", "gz"), None, None),
        P(("gx", "gy", "gz"), None),
        P(("gx", "gy"), None),
        P(("gx", "gy"), None),
    )
    out_specs = P(("gx", "gy", "gz"), None)
    return jax.shard_map(
        on_device, mesh=mesh, in_specs=in_specs, out_specs=out_specs, check_vma=False
    )
```

time: 107 us -> 108 us (level)
  matrix products: 18.6 us -> 0 us
  Pallas kernels: 26.8 us -> 41.6 us
  blocking collectives: 0 us -> 14.6 us
  local copies, waits for them, and re-layouts: 20.9 us -> 13.7 us
  starting transfers between devices: 13.8 us -> 11.7 us
    dot_general x14 -> x0, matrix products: 18.6 us -> none  [the longest x12 14.5 us: transform(): jnp.einsum('ix,jy,kz,nxyz->nijk', filter_table, filter_table, filter_tabl...]
    pallas_call x2 -> x5, Pallas kernels: 26.8 us -> 41.6 us  [the longest x2 28.4 us: images(): pl.pallas_call(functools.partial(kernel, (edge, disp, nodes, padded, tile...]
    all_to_all x0 -> x1, blocking collectives: none -> 14.6 us  [on_device(): lax.all_to_all(coarse_buffer, ('gx', 'gy'), split_axis=0, concat_axis=0,...]
    reshape x16 -> x3, local copies, waits for them, and re-layouts: 10.5 us -> 2.18 us  [the longest x1 1.12 us: on_device(): leaf_coeffs.reshape(nodes, 4, 2, face, order).transpose(0, 1, 3, 2, 4)]
    all_to_all x2 -> x1, starting transfers between devices: 10.1 us -> 6.35 us  [on_device(): lax.all_to_all(jnp.broadcast_to(corners[None], (count_gz,) + corners.shap...]
    all_to_all x2 -> x1, waiting for transfers between devices: 2.96 us -> 0.01 us  [on_device(): lax.all_to_all(jnp.broadcast_to(corners[None], (count_gz,) + corners.shap...]
    all_to_all x1, waiting for transfers between devices: 22.3 us -> 24.9 us  [on_device(): lax.all_to_all(middle_buffer, ('gy', 'gz'), split_axis=0, concat_axis=0,...]
    dot_general x8 -> x0, local copies, waits for them, and re-layouts: 2.32 us -> none  [the longest x5 1.84 us: transform(): jnp.einsum('ix,jy,kz,nxyz->nijk', filter_table, filter_table, filter_tabl...]
  transfers between devices with their start and end apart: 3 -> 2, of which waited for: 2 -> 1; matrix products, arithmetic and copies ran while one was open for 13% -> 6% of each run, Pallas kernels for 13% -> 16%
where the time goes in v2:
time: 108 us; the launch traced here: 107 us
  Pallas kernels  41.6 us (39%)
  waiting for transfers between devices  24.9 us (23%)
  blocking collectives  14.6 us (14%)
  local copies, waits for them, and re-layouts  13.7 us (13%)
  starting transfers between devices  11.7 us (11%)
    pallas_call x2, Pallas kernels, images(): pl.pallas_call(functools.partial(kernel, (edge, disp, nodes, padded, tile...  28.4 us
    all_to_all x1, waiting for transfers between devices, on_device(): lax.all_to_all(middle_buffer, ('gy', 'gz'), split_axis=0, concat_axis=0,...  24.9 us
    all_to_all x1, blocking collectives, on_device(): lax.all_to_all(coarse_buffer, ('gx', 'gy'), split_axis=0, concat_axis=0,...  14.6 us
    all_to_all x1, starting transfers between devices, on_device(): lax.all_to_all(jnp.broadcast_to(corners[None], (count_gz,) + corners.shap...  6.35 us
    all_to_all x1, starting transfers between devices, on_device(): lax.all_to_all(middle_buffer, ('gy', 'gz'), split_axis=0, concat_axis=0,...  5.34 us
    pallas_call x1, Pallas kernels, on_device(): pl.pallas_call(forward_kernel, out_shape=(jax.ShapeDtypeStruct((nodes, ce...  4.64 us
    pallas_call x1, Pallas kernels, on_device(): pl.pallas_call(final_kernel, out_shape=jax.ShapeDtypeStruct((nodes, 4 * b...  4.44 us
    pallas_call x1, Pallas kernels, on_device(): pl.pallas_call(back_kernel, out_shape=jax.ShapeDtypeStruct((nodes, block,...  4.13 us
  transfers between devices with their start and end apart: 2, of which 1 were waited for; matrix products, arithmetic and copies ran while one was open for 6% of the time, Pallas kernels for 16%

profile of v2, /device:TPU:0, one launch (start us, length us, event | category | flops | bytes accessed | tf_op | source)
XLA Modules:
  0.0 107.3 jit_solution(10597645628511237663)
XLA Ops:
  0.0 1.1 %reshape.83 = f32[2,4,2,100,10]{4,3,2,1,0:T(8,128)S(1)} reshape(f32[16,1000]{1,0:T(8,128)} %param.15) | data formatting | bytes 128000 | tf_op jit(solution)/shard_map/reshape | solution.py:315
  1.1 0.3 copy.18
  1.4 0.2 copy.22
  1.7 0.8 pad.11.clone
  2.5 4.6 %shard_map.145 = (f32[2,400,20]{2,1,0:T(8,128)}, f32[2,16,128]{2,1,0:T(8,128)}) custom-call(f32[2,416,20]{2,1,0:T(8,128)} %bitcast.34, bf16[2,528,416]{2,1,0:T(8,128)(2,1)} %constant.29.clone.forward_ref.square_ref, f32[20,20]{1,0:T(8,128)} %constant.30.clone.h_ref, f32[16,20]{1,0:T(8,128)} %constant.31.clone.head_ref), custom_call_target="tpu_custom_call" | custom-call | tf_op jit(solution)/shard_map/pallas_call | solution.py:317
  7.1 1.4 %broadcast_in_dim.2 = f32[4,2,16,128]{3,2,1,0:T(8,128)} broadcast(f32[2,16,128]{2,1,0:T(8,128)} %get-tuple-element.10), dimensions={1,2,3} | broadcast | bytes 81920 | tf_op jit(solution)/shard_map/broadcast_in_dim | solution.py:327
  8.5 6.3 %all-to-all-start = ((f32[8,16,128]{2,1,0:T(8,128)}), f32[8,16,128]{2,1,0:T(8,128)S(1)}, u32[]{:S(2)}, u32[]{:S(2)}) async-start(f32[8,16,128]{2,1,0:T(8,128)} %bitcast.6), calls=%async_computation | async-start | bytes 131072 | tf_op jit(solution)/shard_map/all_to_all | solution.py:326
  15.0 0.2 squeeze.14
  15.2 0.2 mul.34
  15.5 0.7 pad.12.third_ref
  16.2 0.6 reshape_squeeze.12.second_ref
  16.9 0.7 reshape_squeeze.13.first_ref
  17.5 0.2 squeeze.16
  17.8 0.2 mul.38
  18.0 0.8 pad.13.third_ref
  18.8 0.6 reshape_squeeze.14.second_ref
  19.4 0.6 reshape_squeeze.15.first_ref
  20.0 0.6 add.12.dest_ref
  20.6 13.6 %shard_map.146 = f32[32,72,128]{2,1,0:T(8,128)} custom-call(s32[2,7]{1,0:T(2,128)} %add.12.dest_ref, f32[2,400,20]{2,1,0:T(8,128)} %get-tuple-element.9.x_ref, f32[640,20]{1,0:T(8,128)} %pad.12.third_ref, f32[28,400]{1,0:T(8,128)} %reshape_squeeze.12.second_ref, f32[28,400]{1,0:T(8,128)} %reshape_squeeze.13.first_ref), custom_call_target="tpu_custom_call" | custom-call | tf_op jit(solution)/shard_map/pallas_call | solution.py:239
  34.2 0.6 copy-done.2
  34.8 14.8 %shard_map.147 = f32[16,72,128]{2,1,0:T(8,128)} custom-call(s32[2,7]{1,0:T(2,128)} %dest_ref.1, s32[1,8]{1,0:T(1,128)} %place_ref.1, f32[8,16,128]{2,1,0:T(8,128)} %copy-done.2, bf16[2,528,416]{2,1,0:T(8,128)(2,1)} %constant.29.clone.forward_ref.square_ref, f32[2,16,20]{2,1,0:T(8,128)} %constant.32.clone.lane_ref, f32[640,20]{1,0:T(8,128)} %pad.13.third_ref, ...), custom_call_target="tpu_custom_call" | custom-call | tf_op jit(solution)/shard_map/pallas_call | solution.py:239
  49.6 14.6 %all_to_all.15 = f32[16,72,128]{2,1,0:T(8,128)} all-to-all(f32[16,72,128]{2,1,0:T(8,128)} %shard_map.147), channel_id=1, replica_groups=mesh['gx'=2,'gy'=4,'gz'=4] {'gx','gy'}, dimensions={0} | all-to-all | bytes 1179648 | tf_op jit(solution)/shard_map/all_to_all | solution.py:342
  64.2 5.3 %all-to-all-start.1 = ((f32[32,72,128]{2,1,0:T(8,128)}), f32[32,72,128]{2,1,0:T(8,128)S(1)}, u32[]{:S(2)}, u32[]{:S(2)}) async-start(f32[32,72,128]{2,1,0:T(8,128)} %shard_map.146), calls=%async_computation.1 | async-start | bytes 2359296 | tf_op jit(solution)/shard_map/all_to_all | solution.py:336
  69.5 0.6 constant_dynamic-slice_fusion.place_ref
  70.1 4.1 %shard_map.148.parent_ref = f32[2,104,20]{2,1,0:T(8,128)} custom-call(s32[1,2]{1,0:T(1,128)} %constant_dynamic-slice_fusion.place_ref, f32[8,2,72,128]{3,2,1,0:T(8,128)} %bitcast.33, bf16[2,416,432]{2,1,0:T(8,128)(2,1)} %constant.33.clone.inverse_ref, f32[128,20]{1,0:T(8,128)} %constant.34.clone.lane_inverse_ref, f32[2,20,20]{2,1,0:T(8,128)} %constant.35.clone.lane_back_ref), custom_call_target="tpu_custom_call" | custom-call | tf_op jit(solution)/shard_map/pallas_call | solution.py:344
  74.3 24.9 %all-to-all-done.1 = f32[32,72,128]{2,1,0:T(8,128)S(1)} async-done(((f32[32,72,128]{2,1,0:T(8,128)}), f32[32,72,128]{2,1,0:T(8,128)S(1)}, u32[]{:S(2)}, u32[]{:S(2)}) %all-to-all-start.1) | async-done | bytes 1179680 | tf_op jit(solution)/shard_map/all_to_all | solution.py:336
  99.2 1.0 copy-done
  100.2 4.4 %shard_map.149 = f32[2,416,20]{2,1,0:T(8,128)} custom-call(f32[16,2,72,128]{3,2,1,0:T(8,128)} %bitcast.31, f32[2,104,20]{2,1,0:T(8,128)} %shard_map.148.parent_ref, bf16[2,416,432]{2,1,0:T(8,128)(2,1)} %constant.33.clone.inverse_ref, bf16[2,416,104]{2,1,0:T(8,128)(2,1)} %constant.36.clone.inner_ref, f32[128,20]{1,0:T(8,128)} %constant.34.clone.lane_inverse_ref), custom_call_target="tpu_custom_call" | custom-call | tf_op jit(solution)/shard_map/pallas_call | solution.py:354
  104.7 1.2 %copy.20 = f32[2,416,20]{1,0,2:T(2,128)S(1)} copy(f32[2,416,20]{2,1,0:T(8,128)} %shard_map.149) | data formatting | bytes 133120 | tf_op jit(solution)/shard_map/pallas_call | solution.py:354
  105.9 0.2 reshape.89
  106.0 0.4 copy.21
  106.4 0.9 reshape.90
  (23 shorter events, 0.4 us)
Async XLA Ops:
  1.7 13.2 %copy-start.1 = (f32[2,7,4,3,400]{4,2,3,1,0:T(4,128)S(1)}, f32[2,7,4,3,400]{4,2,3,1,0:T(4,128)}, u32[]{:S(2)}) copy-start(f32[2,7,4,3,400]{4,2,3,1,0:T(4,128)} %param.16) | copy-start | bytes 806404
  2.5 12.4 %copy-start.4 = (s32[2,7]{1,0:T(2,128)S(1)}, s32[2,7]{1,0:T(2,128)}, u32[]{:S(2)}) copy-start(s32[2,7]{1,0:T(2,128)} %param.17) | copy-start | bytes 172
  7.1 7.9 %copy-start.5 = (s32[2,7,1]{1,2,0:T(1,128)S(1)}, s32[2,7,1]{1,2,0:T(1,128)}, u32[]{:S(2)}) copy-start(s32[2,7,1]{1,2,0:T(1,128)} %param.18) | copy-start | bytes 172
  8.5 25.7 %all-to-all-start = ((f32[8,16,128]{2,1,0:T(8,128)}), f32[8,16,128]{2,1,0:T(8,128)S(1)}, u32[]{:S(2)}, u32[]{:S(2)}) async-start(f32[8,16,128]{2,1,0:T(8,128)} %bitcast.6), calls=%async_computation | async-start | bytes 131072 | tf_op jit(solution)/shard_map/all_to_all | solution.py:326
  17.5 2.5 %copy-start.3 = (s32[2,7]{1,0:T(2,128)S(1)}, s32[2,7]{1,0:T(2,128)}, u32[]{:S(2)}) copy-start(s32[2,7]{1,0:T(2,128)} %param.19) | copy-start | bytes 172
  34.2 0.6 copy-start.2
  64.2 5.4 %copy-start.6 = (s32[1,8]{1,0:T(1,128)S(1)}, s32[1,8]{1,0:T(1,128)}, u32[]{:S(2)}) copy-start(s32[1,8]{1,0:T(1,128)} %place_ref.1) | copy-start | bytes 100
  64.2 35.0 %all-to-all-start.1 = ((f32[32,72,128]{2,1,0:T(8,128)}), f32[32,72,128]{2,1,0:T(8,128)S(1)}, u32[]{:S(2)}, u32[]{:S(2)}) async-start(f32[32,72,128]{2,1,0:T(8,128)} %shard_map.146), calls=%async_computation.1 | async-start | bytes 2359296 | tf_op jit(solution)/shard_map/all_to_all | solution.py:336
  99.2 1.0 copy-start

commit v3 on v2

--- a/solution.py
+++ b/solution.py
@@ -8,9 +8,11 @@
 from jax.experimental.pallas import tpu as pltpu
 from jax.sharding import PartitionSpec as P
 
+
 ORDER = 10
 LANES = 128
 CHUNK_ROWS = 72
+
 
 def ceil_to(value, step):
     return -(-value // step) * step
@@ -250,12 +252,69 @@
     )(*scalars, *extra, third, second, first)
 
 
-def forward_kernel(leaf_ref, forward_ref, h_ref, head_ref, x_ref, corner_ref):
+def group_place(names):
+    place, size = 0, 1
+    for name in names:
+        place = place * lax.axis_size(name) + lax.axis_index(name)
+        size = size * lax.axis_size(name)
+    return place, size
+
+
+def group_device(names, place):
+    device = {}
+    for name in reversed(names):
+        device[name] = lax.rem(place, lax.axis_size(name))
+        place = place // lax.axis_size(name)
+    return device
+
+
+def greet(names):
+    me, size = group_place(names)
+    barrier = pltpu.get_barrier_semaphore()
+    for step in range(1, size):
+        pl.semaphore_signal(
+            barrier, inc=1, device_id=group_device(names, lax.rem(me + step, size)),
+            device_id_type=pl.DeviceIdType.MESH,
+        )
+    return lambda: pl.semaphore_wait(barrier, size - 1)
+
+
+def group_sends(names, source_of, landed_ref, send_sem, recv_sem):
+    me, size = group_place(names)
+    copies = []
+    for step in range(1, size):
+        to = lax.rem(me + step, size)
+        copies.append(
+            pltpu.make_async_remote_copy(
+                src_ref=source_of(to), dst_ref=landed_ref.at[me],
+                send_sem=send_sem.at[step - 1], recv_sem=recv_sem.at[step - 1],
+                device_id=group_device(names, to), device_id_type=pl.DeviceIdType.MESH,
+            )
+        )
+    return copies
+
+
+def forward_kernel(
+    leaf_ref, forward_ref, h_ref, head_ref, x_ref, column_ref, corner_ref, landed_ref, send_sem, recv_sem
+):
+    names = ("gz",)
+    me, size = group_place(names)
+    greeted = greet(names)
     cells = x_ref.shape[1]
-    for node in range(x_ref.shape[0]):
+    nodes = x_ref.shape[0]
+    for node in range(nodes):
         rows = table_dot(forward_ref, leaf_ref[node])
         x_ref[node] = split_dot(nt_dot, rows[:cells], h_ref[...])
         corner_ref[node] = split_dot(nt_dot, head_ref[...], rows[cells:])
+    greeted()
+    copies = group_sends(names, lambda to: corner_ref, landed_ref, send_sem, recv_sem)
+    for copy in copies:
+        copy.start()
+    column_ref[pl.ds(me, 1)] = corner_ref[...][None]
+    for step, copy in enumerate(copies, 1):
+        copy.wait()
+        source = lax.rem(me + size - step, size)
+        column_ref[pl.ds(source, 1)] = landed_ref[pl.ds(source, 1)]
 
 
 def unpacked(packed, edge, scratch_ref):
@@ -265,15 +324,26 @@
     return scratch_ref[...]
 
 
-def back_kernel(place_ref, arrived_ref, inverse_ref, lane_inverse_ref, lane_back_ref, out_ref, scratch_ref):
-    sources, coarse = arrived_ref.shape[:2]
+def back_kernel(
+    place_ref, buffer_ref, inverse_ref, lane_inverse_ref, lane_back_ref, out_ref,
+    scratch_ref, landed_ref, send_sem, recv_sem,
+):
+    names = ("gx", "gy")
+    me, size = group_place(names)
+    greet(names)()
+    copies = group_sends(names, lambda to: buffer_ref.at[to], landed_ref, send_sem, recv_sem)
+    for copy in copies:
+        copy.start()
+    for copy in copies:
+        copy.wait()
+    coarse = buffer_ref.shape[1]
     edge = out_ref.shape[2]
     block = out_ref.shape[1]
     backs = []
     for p in range(coarse):
-        total = arrived_ref[0, p]
-        for source in range(1, sources):
-            total = total + arrived_ref[source, p]
+        total = buffer_ref[me, p]
+        for step in range(1, size):
+            total = total + landed_ref[lax.rem(me + size - step, size), p]
         lanes = split_dot(nn_dot, unpacked(total, edge, scratch_ref), lane_inverse_ref[...])
         backs.append(table_dot(inverse_ref, lanes))
     for node in range(out_ref.shape[0]):
@@ -314,19 +384,23 @@
 
     leaves = leaf_coeffs.reshape(nodes, 4, 2, face, order).transpose(0, 1, 3, 2, 4)
     leaves = jnp.pad(leaves.reshape(nodes, 4, face, edge), ((0, 0), (0, 0), (0, block - face), (0, 0)))
-    middle, corners = pl.pallas_call(
+    middle, column = pl.pallas_call(
         forward_kernel,
         out_shape=(
             jax.ShapeDtypeStruct((nodes, cells, edge), jnp.float32),
-            jax.ShapeDtypeStruct((nodes, pad, LANES), jnp.float32),
+            jax.ShapeDtypeStruct((count_gz, nodes, pad, LANES), jnp.float32),
         ),
         in_specs=[VMEM] * 4,
         out_specs=(VMEM, VMEM),
+        scratch_shapes=[
+            pltpu.VMEM((nodes, pad, LANES), jnp.float32),
+            pltpu.VMEM((count_gz, nodes, pad, LANES), jnp.float32),
+            pltpu.SemaphoreType.DMA((count_gz,)),
+            pltpu.SemaphoreType.DMA((count_gz,)),
+        ],
+        compiler_params=pltpu.CompilerParams(collective_id=0, has_side_effects=True),
     )(leaves.reshape(nodes, 4 * block, edge), table["forward"], table["h"], table["head"])
-    column = lax.all_to_all(
-        jnp.broadcast_to(corners[None], (count_gz,) + corners.shape).reshape(-1, pad, LANES),
-        "gz", split_axis=0, concat_axis=0, tiled=True,
-    )
+    column = column.reshape(-1, pad, LANES)
     destination = target_device[:, :, 0] * nodes + target_slot
     middle_buffer = images(
         middle_images_kernel, nodes, edge, (destination,), (middle,),
@@ -339,16 +413,21 @@
         (column, table["forward"], table["lane_place"]),
         operator_blocks[0], term_ranks[0], count_gx * count_gy * coarse,
     )
-    arrived = lax.all_to_all(coarse_buffer, ("gx", "gy"), split_axis=0, concat_axis=0, tiled=True)
     own_place = lax.dynamic_slice_in_dim(parent_place, lax.axis_index("gz") * nodes, nodes, 1)
+    plane = count_gx * count_gy
     parent = pl.pallas_call(
         back_kernel,
         out_shape=jax.ShapeDtypeStruct((nodes, block, edge), jnp.float32),
         in_specs=[SMEM] + [VMEM] * 4,
         out_specs=VMEM,
-        scratch_shapes=scratch,
+        scratch_shapes=scratch + [
+            pltpu.VMEM((plane, coarse, CHUNK_ROWS, LANES), jnp.float32),
+            pltpu.SemaphoreType.DMA((plane,)),
+            pltpu.SemaphoreType.DMA((plane,)),
+        ],
+        compiler_params=pltpu.CompilerParams(collective_id=1, has_side_effects=True),
     )(
-        own_place, arrived.reshape(-1, coarse, CHUNK_ROWS, LANES), table["inverse"],
+        own_place, coarse_buffer.reshape(plane, coarse, CHUNK_ROWS, LANES), table["inverse"],
         table["lane_inverse"], table["lane_back"],
     )
     result = pl.pallas_call(

time: 108 us -> 77.2 us (0.71)
  waiting for transfers between devices: 24.9 us -> 0.01 us
  Pallas kernels: 41.6 us -> 59.3 us
  blocking collectives: 14.6 us -> 0 us
  starting transfers between devices: 11.7 us -> 3.92 us
  local copies, waits for them, and re-layouts: 13.7 us -> 11.9 us
    all_to_all x1, waiting for transfers between devices: 24.9 us -> 0.01 us  [on_device(): lax.all_to_all(middle_buffer, ('gy', 'gz'), split_axis=0, concat_axis=0,...]
    all_to_all x1 -> x0, blocking collectives: 14.6 us -> none  [on_device(): lax.all_to_all(coarse_buffer, ('gx', 'gy'), split_axis=0, concat_axis=0,...]
    pallas_call x1, Pallas kernels: 4.13 us -> 14.9 us  [on_device(): pl.pallas_call(back_kernel, out_shape=jax.ShapeDtypeStruct((nodes, block,...]
    pallas_call x1, Pallas kernels: 4.64 us -> 11.6 us  [on_device(): pl.pallas_call(forward_kernel, out_shape=(jax.ShapeDtypeStruct((nodes, ce...]
    all_to_all x1 -> x0, starting transfers between devices: 6.35 us -> none  [on_device(): lax.all_to_all(jnp.broadcast_to(corners[None], (count_gz,) + corners.shap...]
    all_to_all x1, starting transfers between devices: 5.34 us -> 3.92 us  [on_device(): lax.all_to_all(middle_buffer, ('gy', 'gz'), split_axis=0, concat_axis=0,...]
    broadcast_in_dim x1 -> x0, local copies, waits for them, and re-layouts: 1.35 us -> none  [on_device(): jnp.broadcast_to(corners[None], (count_gz,) + corners.shape)]
  transfers between devices with their start and end apart: 2 -> 1, of which waited for: 1 -> 0; matrix products, arithmetic and copies ran while one was open for 6% -> 4% of each run, Pallas kernels for 16% -> 39%
where the time goes in v3:
time: 77.2 us; the launch traced here: 76 us
  Pallas kernels  59.3 us (77%)
  local copies, waits for them, and re-layouts  11.9 us (15%)
  starting transfers between devices  3.92 us (5%)
    pallas_call x2, Pallas kernels, images(): pl.pallas_call(functools.partial(kernel, (edge, disp, nodes, padded, tile...  28.3 us
    pallas_call x1, Pallas kernels, on_device(): pl.pallas_call(back_kernel, out_shape=jax.ShapeDtypeStruct((nodes, block,...  14.9 us
    pallas_call x1, Pallas kernels, on_device(): pl.pallas_call(forward_kernel, out_shape=(jax.ShapeDtypeStruct((nodes, ce...  11.6 us
    pallas_call x1, Pallas kernels, on_device(): pl.pallas_call(final_kernel, out_shape=jax.ShapeDtypeStruct((nodes, 4 * b...  4.46 us
    all_to_all x1, starting transfers between devices, on_device(): lax.all_to_all(middle_buffer, ('gy', 'gz'), split_axis=0, concat_axis=0,...  3.92 us
  transfers between devices with their start and end apart: 1, of which 0 were waited for; matrix products, arithmetic and copies ran while one was open for 4% of the time, Pallas kernels for 39%

profile of v3, /device:TPU:0, one launch (start us, length us, event | category | flops | bytes accessed | tf_op | source)
XLA Modules:
  0.0 76.0 jit_solution(2705303808455947975)
XLA Ops:
  0.0 1.1 %slice_bitcast_fusion = (f32[7,4,3,400]{3,1,2,0:T(4,128)S(1)}, f32[7,4,3,400]{3,1,2,0:T(4,128)S(1)}) fusion(f32[2,7,4,3,400]{4,2,3,1,0:T(4,128)} %param.16), kind=kLoop, calls=%fused_computation | loop fusion | bytes 537600 | tf_op jit(solution)/shard_map/squeeze | solution.py:414
  1.1 0.2 squeeze.14
  1.3 0.1 fusion
  1.4 0.1 mul.33
  1.4 0.2 mul.34
  1.6 0.7 reshape_squeeze.12.second_ref
  2.3 0.6 reshape_squeeze.13.first_ref
  2.9 0.3 reshape.82
  3.2 0.3 copy.18
  3.5 0.2 copy.22
  3.8 0.0 copy-start.2
  3.8 0.7 pad.12.third_ref
  4.6 0.8 %pad.11.clone = f32[2,4,104,20]{3,2,1,0:T(8,128)} pad(f32[2,4,100,20]{3,2,1,0:T(8,128)S(1)} %copy.22, f32[]{:T(128)} %constant.10.clone.1), padding=0_0x0_0x0_4x0_0 | pad | bytes 130564 | tf_op jit(solution)/shard_map/jit(_pad)/pad | solution.py:386
  5.4 0.6 add.12.dest_ref
  6.0 11.6 %shard_map.145 = (f32[2,400,20]{2,1,0:T(8,128)}, f32[4,2,16,128]{3,2,1,0:T(8,128)}) custom-call(f32[2,416,20]{2,1,0:T(8,128)} %bitcast.34, bf16[2,528,416]{2,1,0:T(8,128)(2,1)} %constant.29.clone.forward_ref.square_ref, f32[20,20]{1,0:T(8,128)} %constant.30.clone.h_ref, f32[16,20]{1,0:T(8,128)} %constant.31.clone.head_ref), custom_call_target="tpu_custom_call" | custom-call | tf_op jit(solution)/shard_map/pallas_call | solution.py:387
  17.6 13.6 %shard_map.146 = f32[32,72,128]{2,1,0:T(8,128)} custom-call(s32[2,7]{1,0:T(2,128)} %add.12.dest_ref, f32[2,400,20]{2,1,0:T(8,128)} %get-tuple-element.9.x_ref, f32[640,20]{1,0:T(8,128)} %pad.12.third_ref, f32[28,400]{1,0:T(8,128)} %reshape_squeeze.12.second_ref, f32[28,400]{1,0:T(8,128)} %reshape_squeeze.13.first_ref), custom_call_target="tpu_custom_call" | custom-call | tf_op jit(solution)/shard_map/pallas_call | solution.py:241
  31.1 3.9 %all-to-all-start = ((f32[32,72,128]{2,1,0:T(8,128)}), f32[32,72,128]{2,1,0:T(8,128)S(1)}, u32[]{:S(2)}, u32[]{:S(2)}) async-start(f32[32,72,128]{2,1,0:T(8,128)} %shard_map.146), calls=%async_computation | async-start | bytes 2359296 | tf_op jit(solution)/shard_map/all_to_all | solution.py:410
  35.1 0.2 squeeze.16
  35.3 0.1 mul.37
  35.3 0.2 mul.38
  35.6 0.8 %pad.13.third_ref = f32[640,20]{1,0:T(8,128)} pad(f32[560,20]{1,0:T(8,128)S(1)} %mul.39, f32[]{:T(128)} %constant.10.clone.1), padding=0_80x0_0 | pad | bytes 96004 | tf_op jit(solution)/shard_map/jit(_pad)/pad | solution.py:237
  36.3 0.6 reshape_squeeze.14.second_ref
  37.0 0.6 reshape_squeeze.15.first_ref
  37.6 14.8 %shard_map.147 = f32[16,72,128]{2,1,0:T(8,128)} custom-call(s32[2,7]{1,0:T(2,128)} %dest_ref.1, s32[1,8]{1,0:T(1,128)} %place_ref.1, f32[8,16,128]{2,1,0:T(8,128)} %bitcast.36, bf16[2,528,416]{2,1,0:T(8,128)(2,1)} %constant.29.clone.forward_ref.square_ref, f32[2,16,20]{2,1,0:T(8,128)} %constant.32.clone.lane_ref, f32[640,20]{1,0:T(8,128)} %pad.13.third_ref, ...), custom_call_target="tpu_custom_call" | custom-call | tf_op jit(solution)/shard_map/pallas_call | solution.py:241
  52.4 0.6 constant_dynamic-slice_fusion.place_ref
  53.0 14.9 %shard_map.148.parent_ref = f32[2,104,20]{2,1,0:T(8,128)} custom-call(s32[1,2]{1,0:T(1,128)} %constant_dynamic-slice_fusion.place_ref, f32[8,2,72,128]{3,2,1,0:T(8,128)} %bitcast.33, bf16[2,416,432]{2,1,0:T(8,128)(2,1)} %constant.33.clone.inverse_ref, f32[128,20]{1,0:T(8,128)} %constant.34.clone.lane_inverse_ref, f32[2,20,20]{2,1,0:T(8,128)} %constant.35.clone.lane_back_ref), custom_call_target="tpu_custom_call" | custom-call | tf_op jit(solution)/shard_map/pallas_call | solution.py:418
  67.9 1.0 %copy-done = f32[32,72,128]{2,1,0:T(8,128)} copy-done((f32[32,72,128]{2,1,0:T(8,128)}, f32[32,72,128]{2,1,0:T(8,128)S(1)}, u32[]{:S(2)}) %copy-start) | copy-done | bytes 1179672
  68.9 4.5 %shard_map.149 = f32[2,416,20]{2,1,0:T(8,128)} custom-call(f32[16,2,72,128]{3,2,1,0:T(8,128)} %bitcast.31, f32[2,104,20]{2,1,0:T(8,128)} %shard_map.148.parent_ref, bf16[2,416,432]{2,1,0:T(8,128)(2,1)} %constant.33.clone.inverse_ref, bf16[2,416,104]{2,1,0:T(8,128)(2,1)} %constant.36.clone.inner_ref, f32[128,20]{1,0:T(8,128)} %constant.34.clone.lane_inverse_ref), custom_call_target="tpu_custom_call" | custom-call | tf_op jit(solution)/shard_map/pallas_call | solution.py:433
  73.4 1.2 %copy.20 = f32[2,416,20]{1,0,2:T(2,128)S(1)} copy(f32[2,416,20]{2,1,0:T(8,128)} %shard_map.149) | data formatting | bytes 133120 | tf_op jit(solution)/shard_map/pallas_call | solution.py:433
  74.6 0.2 reshape.88
  74.7 0.4 copy.21
  75.1 0.9 %reshape.89 = f32[16,1000]{1,0:T(8,128)} reshape(f32[2,4,2,100,10]{4,3,2,1,0:T(8,128)S(1)} %copy.21) | data formatting | bytes 128000 | tf_op jit(solution)/shard_map/reshape | solution.py:444
  (17 shorter events, 0.2 us)
Async XLA Ops:
  0.0 1.3 %copy-start.3 = (s32[2,7]{1,0:T(2,128)S(1)}, s32[2,7]{1,0:T(2,128)}, u32[]{:S(2)}) copy-start(s32[2,7]{1,0:T(2,128)} %param.17) | copy-start | bytes 172
  0.0 2.9 %copy-start.1 = (f32[16,1000]{1,0:T(8,128)S(1)}, f32[16,1000]{1,0:T(8,128)}, u32[]{:S(2)}) copy-start(f32[16,1000]{1,0:T(8,128)} %param.15) | copy-start | bytes 192004
  3.8 1.6 %copy-start.4 = (s32[2,7,1]{1,2,0:T(1,128)S(1)}, s32[2,7,1]{1,2,0:T(1,128)}, u32[]{:S(2)}) copy-start(s32[2,7,1]{1,2,0:T(1,128)} %param.18) | copy-start | bytes 172
  3.8 1.6 %copy-start.2 = (s32[2,7]{1,0:T(2,128)S(1)}, s32[2,7]{1,0:T(2,128)}, u32[]{:S(2)}) copy-start(s32[2,7]{1,0:T(2,128)} %param.19) | copy-start | bytes 172
  31.1 36.7 %all-to-all-start = ((f32[32,72,128]{2,1,0:T(8,128)}), f32[32,72,128]{2,1,0:T(8,128)S(1)}, u32[]{:S(2)}, u32[]{:S(2)}) async-start(f32[32,72,128]{2,1,0:T(8,128)} %shard_map.146), calls=%async_computation | async-start | bytes 2359296 | tf_op jit(solution)/shard_map/all_to_all | solution.py:410
  37.0 15.4 %copy-start.5 = (s32[1,8]{1,0:T(1,128)S(1)}, s32[1,8]{1,0:T(1,128)}, u32[]{:S(2)}) copy-start(s32[1,8]{1,0:T(1,128)} %place_ref.1) | copy-start | bytes 100
  67.9 1.0 %copy-start = (f32[32,72,128]{2,1,0:T(8,128)}, f32[32,72,128]{2,1,0:T(8,128)S(1)}, u32[]{:S(2)}) copy-start(f32[32,72,128]{2,1,0:T(8,128)S(1)} %all-to-all-done) | copy-start | bytes 3538948

commit v4 on v3

--- a/solution.py
+++ b/solution.py
@@ -95,10 +95,10 @@
 
 def images_body(
     edge, disp, nodes, padded, tiles, block_of,
-    dest_ref, third_ref, second_ref, first_ref, out_ref,
+    level, dest_ref, third_ref, factors_ref, out_ref,
     ping_ref, pong_ref, coef_ref, image_ref,
 ):
-    pairs = first_ref.shape[0]
+    pairs = factors_ref.shape[2]
     width = tiles * LANES
     rows = padded * edge
     spread = (
@@ -106,8 +106,7 @@
         == lax.broadcasted_iota(jnp.int32, (pairs, width), 0)
     ).astype(jnp.bfloat16)
 
-    def fill(slot, source_ref):
-        value = source_ref[...]
+    def fill(slot, value):
         high = value.astype(jnp.bfloat16)
         rest = value - high.astype(jnp.float32)
         mid, low = halves(rest)
@@ -115,9 +114,9 @@
         for tile in range(tiles):
             coef_ref[slot, tile] = table[:, tile * LANES:(tile + 1) * LANES]
 
-    fill(0, second_ref)
-    fill(1, first_ref)
-    w_high, w_low = halves(third_ref[...])
+    fill(0, factors_ref[level, 1])
+    fill(1, factors_ref[level, 0])
+    w_high, w_low = halves(third_ref[level])
     cells = edge * edge
     for node in range(padded):
         at = slice(node * cells, (node + 1) * cells)
@@ -195,13 +194,12 @@
             out_ref[to] = out_ref[to] + packed
 
 
-def middle_images_kernel(sizes, dest_ref, x_ref, third_ref, second_ref, first_ref, *rest):
-    images_body(*sizes, lambda node: x_ref[node], dest_ref, third_ref, second_ref, first_ref, *rest)
+def middle_images_kernel(sizes, dest_ref, x_ref, *rest):
+    images_body(*sizes, lambda node: x_ref[node], 1, dest_ref, *rest)
 
 
 def coarse_images_kernel(
-    sizes, dest_ref, place_ref, column_ref, square_ref, lane_ref,
-    third_ref, second_ref, first_ref, *rest,
+    sizes, dest_ref, place_ref, column_ref, square_ref, lane_ref, *rest
 ):
     members = column_ref.shape[0]
     block = square_ref.shape[2] // 4
@@ -220,28 +218,32 @@
             parts.append(part)
         return table_dot(square_ref, jnp.concatenate(parts, axis=0), spread[0].shape[1] ** 2)
 
-    images_body(*sizes, block_of, dest_ref, third_ref, second_ref, first_ref, *rest)
+    images_body(*sizes, block_of, 0, dest_ref, *rest)
 
 
 VMEM = pl.BlockSpec(memory_space=pltpu.VMEM)
 SMEM = pl.BlockSpec(memory_space=pltpu.SMEM)
 
 
-def images(kernel, nodes, edge, scalars, extra, matrices, ranks, buffer_rows):
-    disp, terms = matrices.shape[0], matrices.shape[1]
+def factor_operands(operator_blocks, ranks, edge):
+    levels, disp, terms = operator_blocks.shape[:3]
     pairs = disp * terms
+    width = ceil_to(pairs * edge, LANES)
+    keep = (jnp.arange(terms, dtype=jnp.int32) < ranks[:, :, None]).astype(jnp.float32)
+    third = (operator_blocks[:, :, :, 2] * keep[..., None]).reshape(levels, pairs * edge, edge)
+    third = jnp.pad(third, ((0, 0), (0, width - pairs * edge), (0, 0)))
+    factors = operator_blocks[:, :, :, :2].transpose(0, 3, 1, 2, 4)
+    return third, factors.reshape(levels, 2, pairs, edge * edge)
+
+
+def images(kernel, nodes, edge, disp, scalars, extra, operands, buffer_rows):
     padded = nodes + nodes % 2
-    tiles = -(-pairs * edge // LANES)
-    keep = (jnp.arange(terms, dtype=jnp.int32)[None, :] < ranks[:, None]).astype(jnp.float32)
-    third = (matrices[:, :, 2] * keep[:, :, None]).reshape(pairs * edge, edge)
-    third = jnp.pad(third, ((0, tiles * LANES - pairs * edge), (0, 0)))
-    second = matrices[:, :, 1].reshape(pairs, edge * edge)
-    first = matrices[:, :, 0].reshape(pairs, edge * edge)
+    tiles = operands[0].shape[1] // LANES
     per_tile = LANES // edge
     return pl.pallas_call(
         functools.partial(kernel, (edge, disp, nodes, padded, tiles)),
         out_shape=jax.ShapeDtypeStruct((buffer_rows, CHUNK_ROWS, LANES), jnp.float32),
-        in_specs=[SMEM] * len(scalars) + [VMEM] * (len(extra) + 3),
+        in_specs=[SMEM] * len(scalars) + [VMEM] * (len(extra) + 2),
         out_specs=VMEM,
         scratch_shapes=[
             pltpu.VMEM((tiles, padded * edge * edge, LANES), jnp.float32),
@@ -249,7 +251,7 @@
             pltpu.VMEM((2, tiles, edge * edge, LANES), jnp.float32),
             pltpu.VMEM((2, padded * CHUNK_ROWS * per_tile, LANES), jnp.float32),
         ],
-    )(*scalars, *extra, third, second, first)
+    )(*scalars, *extra, *operands)
 
 
 def group_place(names):
@@ -294,19 +296,18 @@
     return copies
 
 
-def forward_kernel(
-    leaf_ref, forward_ref, h_ref, head_ref, x_ref, column_ref, corner_ref, landed_ref, send_sem, recv_sem
-):
-    names = ("gz",)
-    me, size = group_place(names)
-    greeted = greet(names)
+def forward_kernel(leaf_ref, forward_ref, h_ref, head_ref, x_ref, corner_ref):
     cells = x_ref.shape[1]
-    nodes = x_ref.shape[0]
-    for node in range(nodes):
+    for node in range(x_ref.shape[0]):
         rows = table_dot(forward_ref, leaf_ref[node])
         x_ref[node] = split_dot(nt_dot, rows[:cells], h_ref[...])
         corner_ref[node] = split_dot(nt_dot, head_ref[...], rows[cells:])
-    greeted()
+
+
+def corner_kernel(corner_ref, column_ref, landed_ref, send_sem, recv_sem):
+    names = ("gz",)
+    me, size = group_place(names)
+    greet(names)()
     copies = group_sends(names, lambda to: corner_ref, landed_ref, send_sem, recv_sem)
     for copy in copies:
         copy.start()
@@ -382,36 +383,42 @@
     pad = table["head"].shape[0]
     scratch = [pltpu.VMEM((LANES // edge * CHUNK_ROWS, LANES), jnp.float32)]
 
+    disp = operator_blocks.shape[1]
+    operands = factor_operands(operator_blocks, term_ranks, edge)
     leaves = leaf_coeffs.reshape(nodes, 4, 2, face, order).transpose(0, 1, 3, 2, 4)
     leaves = jnp.pad(leaves.reshape(nodes, 4, face, edge), ((0, 0), (0, 0), (0, block - face), (0, 0)))
-    middle, column = pl.pallas_call(
+    middle, corners = pl.pallas_call(
         forward_kernel,
         out_shape=(
             jax.ShapeDtypeStruct((nodes, cells, edge), jnp.float32),
-            jax.ShapeDtypeStruct((count_gz, nodes, pad, LANES), jnp.float32),
+            jax.ShapeDtypeStruct((nodes, pad, LANES), jnp.float32),
         ),
         in_specs=[VMEM] * 4,
         out_specs=(VMEM, VMEM),
+    )(leaves.reshape(nodes, 4 * block, edge), table["forward"], table["h"], table["head"])
+    destination = target_device[:, :, 0] * nodes + target_slot
+    middle_buffer = images(
+        middle_images_kernel, nodes, edge, disp, (destination,), (middle,),
+        operands, count_gy * count_gz * nodes,
+    )
+    middle_buffer, corners = lax.optimization_barrier((middle_buffer, corners))
+    received = lax.all_to_all(middle_buffer, ("gy", "gz"), split_axis=0, concat_axis=0, tiled=True)
+    column = pl.pallas_call(
+        corner_kernel,
+        out_shape=jax.ShapeDtypeStruct((count_gz, nodes, pad, LANES), jnp.float32),
+        in_specs=[VMEM],
+        out_specs=VMEM,
         scratch_shapes=[
-            pltpu.VMEM((nodes, pad, LANES), jnp.float32),
             pltpu.VMEM((count_gz, nodes, pad, LANES), jnp.float32),
             pltpu.SemaphoreType.DMA((count_gz,)),
             pltpu.SemaphoreType.DMA((count_gz,)),
         ],
         compiler_params=pltpu.CompilerParams(collective_id=0, has_side_effects=True),
-    )(leaves.reshape(nodes, 4 * block, edge), table["forward"], table["h"], table["head"])
-    column = column.reshape(-1, pad, LANES)
-    destination = target_device[:, :, 0] * nodes + target_slot
-    middle_buffer = images(
-        middle_images_kernel, nodes, edge, (destination,), (middle,),
-        operator_blocks[1], term_ranks[1], count_gy * count_gz * nodes,
-    )
-    middle_buffer, column = lax.optimization_barrier((middle_buffer, column))
-    received = lax.all_to_all(middle_buffer, ("gy", "gz"), split_axis=0, concat_axis=0, tiled=True)
+    )(corners).reshape(-1, pad, LANES)
     coarse_buffer = images(
-        coarse_images_kernel, coarse, edge, (coarse_targets, parent_place),
+        coarse_images_kernel, coarse, edge, disp, (coarse_targets, parent_place),
         (column, table["forward"], table["lane_place"]),
-        operator_blocks[0], term_ranks[0], count_gx * count_gy * coarse,
+        operands, count_gx * count_gy * coarse,
     )
     own_place = lax.dynamic_slice_in_dim(parent_place, lax.axis_index("gz") * nodes, nodes, 1)
     plane = count_gx * count_gy

time: 77.2 us -> 102 us (1.32)
  Pallas kernels: 59.3 us -> 82.7 us
  starting transfers between devices: 3.92 us -> 7.39 us
  local copies, waits for them, and re-layouts: 11.9 us -> 9.39 us
    pallas_call x0 -> x1, Pallas kernels: none -> 31.2 us  [on_device(): pl.pallas_call(corner_kernel, out_shape=jax.ShapeDtypeStruct((count_gz, n...]
    pallas_call x1, Pallas kernels: 11.6 us -> 4.64 us  [on_device(): pl.pallas_call(forward_kernel, out_shape=(jax.ShapeDtypeStruct((nodes, ce...]
    all_to_all x1, starting transfers between devices: 3.92 us -> 7.39 us  [on_device(): lax.all_to_all(middle_buffer, ('gy', 'gz'), split_axis=0, concat_axis=0,...]
    another operation x4 -> x0, local copies, waits for them, and re-layouts: 2.58 us -> none  [the longest x2 1.3 us: images(): second = matrices[:, :, 1].reshape(pairs, edge * edge)]
    pallas_call x1, Pallas kernels: 14.9 us -> 13.7 us  [on_device(): pl.pallas_call(back_kernel, out_shape=jax.ShapeDtypeStruct((nodes, block,...]
    transpose x0 -> x2, local copies, waits for them, and re-layouts: none -> 1.11 us  [factor_operands(): factors = operator_blocks[:, :, :, :2].transpose(0, 3, 1, 2, 4)]
    squeeze x3 -> x1, local copies, waits for them, and re-layouts: 1.4 us -> 0.34 us  [factor_operands(): operator_blocks[:, :, :, 2] * keep[..., None]]
  transfers between devices with their start and end apart: 1 -> 1, of which waited for: 0 -> 0; matrix products, arithmetic and copies ran while one was open for 4% -> 1% of each run, Pallas kernels for 39% -> 59%
where the time goes in v4:
time: 102 us; the launch traced here: 101 us
  Pallas kernels  82.7 us (81%)
  local copies, waits for them, and re-layouts  9.39 us (9%)
  starting transfers between devices  7.39 us (7%)
  other arithmetic  1.38 us (1%)
    pallas_call x1, Pallas kernels, on_device(): pl.pallas_call(corner_kernel, out_shape=jax.ShapeDtypeStruct((count_gz, n...  31.2 us
    pallas_call x2, Pallas kernels, images(): pl.pallas_call(functools.partial(kernel, (edge, disp, nodes, padded, tile...  28.7 us
    pallas_call x1, Pallas kernels, on_device(): pl.pallas_call(back_kernel, out_shape=jax.ShapeDtypeStruct((nodes, block,...  13.7 us
    all_to_all x1, starting transfers between devices, on_device(): lax.all_to_all(middle_buffer, ('gy', 'gz'), split_axis=0, concat_axis=0,...  7.39 us
    pallas_call x1, Pallas kernels, on_device(): pl.pallas_call(forward_kernel, out_shape=(jax.ShapeDtypeStruct((nodes, ce...  4.64 us
    pallas_call x1, Pallas kernels, on_device(): pl.pallas_call(final_kernel, out_shape=jax.ShapeDtypeStruct((nodes, 4 * b...  4.46 us
  transfers between devices with their start and end apart: 1, of which 0 were waited for; matrix products, arithmetic and copies ran while one was open for 1% of the time, Pallas kernels for 59%

profile of v4, /device:TPU:0, one launch (start us, length us, event | category | flops | bytes accessed | tf_op | source)
XLA Modules:
  0.0 101.0 jit_solution(4987601239067117413)
XLA Ops:
  0.0 1.0 slice_bitcast_fusion
  1.0 0.8 fusion
  1.8 0.1 mul.22
  1.8 0.3 mul.23
  2.2 0.0 slice-done
  2.2 0.3 squeeze.4
  2.5 0.0 copy-done.1
  2.6 0.3 reshape.37
  2.8 0.3 copy.19
  3.2 0.2 copy.26
  3.4 0.1 mul.24
  3.5 0.9 pad.9.rest_0_
  4.4 0.8 pad.8.clone
  5.2 0.1 copy.21
  5.3 0.7 copy.22.rest_1_
  6.0 0.0 copy-done.3
  6.0 0.6 add.10.dest_ref
  6.6 4.6 %shard_map.145 = (f32[2,400,20]{2,1,0:T(8,128)}, f32[2,16,128]{2,1,0:T(8,128)}) custom-call(f32[2,416,20]{2,1,0:T(8,128)} %bitcast.19, bf16[2,528,416]{2,1,0:T(8,128)(2,1)} %constant.29.clone.forward_ref.square_ref, f32[20,20]{1,0:T(8,128)} %constant.30.clone.h_ref, f32[16,20]{1,0:T(8,128)} %constant.31.clone.head_ref), custom_call_target="tpu_custom_call" | custom-call | tf_op jit(solution)/shard_map/pallas_call | solution.py:390
  11.3 13.7 %shard_map.146 = f32[32,72,128]{2,1,0:T(8,128)} custom-call(s32[2,7]{1,0:T(2,128)} %add.10.dest_ref, f32[2,400,20]{2,1,0:T(8,128)} %get-tuple-element.9.x_ref, f32[2,640,20]{2,1,0:T(8,128)} %pad.9.rest_0_, f32[2,2,28,400]{3,2,1,0:T(8,128)} %copy.22.rest_1_), custom_call_target="tpu_custom_call" | custom-call | tf_op jit(solution)/shard_map/pallas_call | solution.py:243
  25.0 7.4 %all-to-all-start = ((f32[32,72,128]{2,1,0:T(8,128)}), f32[32,72,128]{2,1,0:T(8,128)S(1)}, u32[]{:S(2)}, u32[]{:S(2)}) async-start(f32[32,72,128]{2,1,0:T(8,128)} %shard_map.146), calls=%async_computation | async-start | bytes 2359296 | tf_op jit(solution)/shard_map/all_to_all | solution.py:405
  32.4 31.2 %shard_map.147 = f32[4,2,16,128]{3,2,1,0:T(8,128)} custom-call(f32[2,16,128]{2,1,0:T(8,128)} %get-tuple-element.12.corner_ref), custom_call_target="tpu_custom_call" | custom-call | tf_op jit(solution)/shard_map/pallas_call | solution.py:406
  63.6 0.0 copy-start.4
  63.6 15.0 %shard_map.148 = f32[16,72,128]{2,1,0:T(8,128)} custom-call(s32[2,7]{1,0:T(2,128)} %dest_ref.1, s32[1,8]{1,0:T(1,128)} %place_ref.1, f32[8,16,128]{2,1,0:T(8,128)} %bitcast.22, bf16[2,528,416]{2,1,0:T(8,128)(2,1)} %constant.29.clone.forward_ref.square_ref, f32[2,16,20]{2,1,0:T(8,128)} %constant.32.clone.lane_ref, f32[2,640,20]{2,1,0:T(8,128)} %pad.9.rest_0_, ...), custom_call_target="tpu_custom_call" | custom-call | tf_op jit(solution)/shard_map/pallas_call | solution.py:243
  78.6 0.6 constant_dynamic-slice_fusion.place_ref
  79.2 13.7 %shard_map.149.parent_ref = f32[2,104,20]{2,1,0:T(8,128)} custom-call(s32[1,2]{1,0:T(1,128)} %constant_dynamic-slice_fusion.place_ref, f32[8,2,72,128]{3,2,1,0:T(8,128)} %bitcast.18, bf16[2,416,432]{2,1,0:T(8,128)(2,1)} %constant.33.clone.inverse_ref, f32[128,20]{1,0:T(8,128)} %constant.34.clone.lane_inverse_ref, f32[2,20,20]{2,1,0:T(8,128)} %constant.35.clone.lane_back_ref), custom_call_target="tpu_custom_call" | custom-call | tf_op jit(solution)/shard_map/pallas_call | solution.py:425
  92.9 0.0 all-to-all-done
  92.9 1.0 %copy-done = f32[32,72,128]{2,1,0:T(8,128)} copy-done((f32[32,72,128]{2,1,0:T(8,128)}, f32[32,72,128]{2,1,0:T(8,128)S(1)}, u32[]{:S(2)}) %copy-start) | copy-done | bytes 1179672
  93.9 4.5 %shard_map.150 = f32[2,416,20]{2,1,0:T(8,128)} custom-call(f32[16,2,72,128]{3,2,1,0:T(8,128)} %bitcast.16, f32[2,104,20]{2,1,0:T(8,128)} %shard_map.149.parent_ref, bf16[2,416,432]{2,1,0:T(8,128)(2,1)} %constant.33.clone.inverse_ref, bf16[2,416,104]{2,1,0:T(8,128)(2,1)} %constant.36.clone.inner_ref, f32[128,20]{1,0:T(8,128)} %constant.34.clone.lane_inverse_ref), custom_call_target="tpu_custom_call" | custom-call | tf_op jit(solution)/shard_map/pallas_call | solution.py:440
  98.4 1.2 %copy.24 = f32[2,416,20]{1,0,2:T(2,128)S(1)} copy(f32[2,416,20]{2,1,0:T(8,128)} %shard_map.150) | data formatting | bytes 133120 | tf_op jit(solution)/shard_map/pallas_call | solution.py:440
  99.6 0.2 reshape.44
  99.8 0.4 copy.25
  100.1 0.9 reshape.45
  (9 shorter events, 0.0 us)
Async XLA Ops:
  0.0 2.2 %slice-start = ((f32[2,7,4,3,400]{4,2,3,1,0:T(4,128)}), f32[2,7,4,1,400]{4,2,3,1,0:T(4,128)S(1)}, s32[]{:S(2)}) async-start(f32[2,7,4,3,400]{4,2,3,1,0:T(4,128)} %param.16), calls=%async_computation.1 | async-start | bytes 229376 | tf_op jit(solution)/shard_map/slice | solution.py:233
  0.0 2.5 %copy-start.1 = (f32[16,1000]{1,0:T(8,128)S(1)}, f32[16,1000]{1,0:T(8,128)}, u32[]{:S(2)}) copy-start(f32[16,1000]{1,0:T(8,128)} %param.15) | copy-start | bytes 192004
  4.4 1.7 %copy-start.3 = (s32[2,7,1]{1,2,0:T(1,128)S(1)}, s32[2,7,1]{1,2,0:T(1,128)}, u32[]{:S(2)}) copy-start(s32[2,7,1]{1,2,0:T(1,128)} %param.18) | copy-start | bytes 172
  4.4 1.7 %copy-start.2 = (s32[2,7]{1,0:T(2,128)S(1)}, s32[2,7]{1,0:T(2,128)}, u32[]{:S(2)}) copy-start(s32[2,7]{1,0:T(2,128)} %param.19) | copy-start | bytes 172
  25.0 67.9 %all-to-all-start = ((f32[32,72,128]{2,1,0:T(8,128)}), f32[32,72,128]{2,1,0:T(8,128)S(1)}, u32[]{:S(2)}, u32[]{:S(2)}) async-start(f32[32,72,128]{2,1,0:T(8,128)} %shard_map.146), calls=%async_computation | async-start | bytes 2359296 | tf_op jit(solution)/shard_map/all_to_all | solution.py:405
  63.6 15.0 %copy-start.4 = (s32[1,8]{1,0:T(1,128)S(1)}, s32[1,8]{1,0:T(1,128)}, u32[]{:S(2)}) copy-start(s32[1,8]{1,0:T(1,128)} %place_ref.1) | copy-start | bytes 100
  92.9 1.0 %copy-start = (f32[32,72,128]{2,1,0:T(8,128)}, f32[32,72,128]{2,1,0:T(8,128)S(1)}, u32[]{:S(2)}) copy-start(f32[32,72,128]{2,1,0:T(8,128)S(1)} %all-to-all-done) | copy-start | bytes 3538948

commit v5 on v4

--- a/solution.py
+++ b/solution.py
@@ -296,18 +296,19 @@
     return copies
 
 
-def forward_kernel(leaf_ref, forward_ref, h_ref, head_ref, x_ref, corner_ref):
+def forward_kernel(
+    leaf_ref, forward_ref, h_ref, head_ref, x_ref, column_ref, corner_ref, landed_ref, send_sem, recv_sem
+):
+    names = ("gz",)
+    me, size = group_place(names)
+    greeted = greet(names)
     cells = x_ref.shape[1]
-    for node in range(x_ref.shape[0]):
+    nodes = x_ref.shape[0]
+    for node in range(nodes):
         rows = table_dot(forward_ref, leaf_ref[node])
         x_ref[node] = split_dot(nt_dot, rows[:cells], h_ref[...])
         corner_ref[node] = split_dot(nt_dot, head_ref[...], rows[cells:])
-
-
-def corner_kernel(corner_ref, column_ref, landed_ref, send_sem, recv_sem):
-    names = ("gz",)
-    me, size = group_place(names)
-    greet(names)()
+    greeted()
     copies = group_sends(names, lambda to: corner_ref, landed_ref, send_sem, recv_sem)
     for copy in copies:
         copy.start()
@@ -387,34 +388,30 @@
     operands = factor_operands(operator_blocks, term_ranks, edge)
     leaves = leaf_coeffs.reshape(nodes, 4, 2, face, order).transpose(0, 1, 3, 2, 4)
     leaves = jnp.pad(leaves.reshape(nodes, 4, face, edge), ((0, 0), (0, 0), (0, block - face), (0, 0)))
-    middle, corners = pl.pallas_call(
+    middle, column = pl.pallas_call(
         forward_kernel,
         out_shape=(
             jax.ShapeDtypeStruct((nodes, cells, edge), jnp.float32),
-            jax.ShapeDtypeStruct((nodes, pad, LANES), jnp.float32),
+            jax.ShapeDtypeStruct((count_gz, nodes, pad, LANES), jnp.float32),
         ),
         in_specs=[VMEM] * 4,
         out_specs=(VMEM, VMEM),
-    )(leaves.reshape(nodes, 4 * block, edge), table["forward"], table["h"], table["head"])
-    destination = target_device[:, :, 0] * nodes + target_slot
-    middle_buffer = images(
-        middle_images_kernel, nodes, edge, disp, (destination,), (middle,),
-        operands, count_gy * count_gz * nodes,
-    )
-    middle_buffer, corners = lax.optimization_barrier((middle_buffer, corners))
-    received = lax.all_to_all(middle_buffer, ("gy", "gz"), split_axis=0, concat_axis=0, tiled=True)
-    column = pl.pallas_call(
-        corner_kernel,
-        out_shape=jax.ShapeDtypeStruct((count_gz, nodes, pad, LANES), jnp.float32),
-        in_specs=[VMEM],
-        out_specs=VMEM,
         scratch_shapes=[
+            pltpu.VMEM((nodes, pad, LANES), jnp.float32),
             pltpu.VMEM((count_gz, nodes, pad, LANES), jnp.float32),
             pltpu.SemaphoreType.DMA((count_gz,)),
             pltpu.SemaphoreType.DMA((count_gz,)),
         ],
         compiler_params=pltpu.CompilerParams(collective_id=0, has_side_effects=True),
-    )(corners).reshape(-1, pad, LANES)
+    )(leaves.reshape(nodes, 4 * block, edge), table["forward"], table["h"], table["head"])
+    column = column.reshape(-1, pad, LANES)
+    destination = target_device[:, :, 0] * nodes + target_slot
+    middle_buffer = images(
+        middle_images_kernel, nodes, edge, disp, (destination,), (middle,),
+        operands, count_gy * count_gz * nodes,
+    )
+    middle_buffer, column = lax.optimization_barrier((middle_buffer, column))
+    received = lax.all_to_all(middle_buffer, ("gy", "gz"), split_axis=0, concat_axis=0, tiled=True)
     coarse_buffer = images(
         coarse_images_kernel, coarse, edge, disp, (coarse_targets, parent_place),
         (column, table["forward"], table["lane_place"]),

time: 102 us -> 76.5 us (0.75)
  the two profiles are of different devices: /device:TPU:0 before, /device:TPU:17 now
where the time goes in v5:
time: 76.5 us; the launch traced here: 76.1 us
  Pallas kernels  58.5 us (76%)
  local copies, waits for them, and re-layouts  9.39 us (12%)
  starting transfers between devices  6.67 us (9%)
  other arithmetic  1.38 us (2%)
    pallas_call x2, Pallas kernels, images(): pl.pallas_call(functools.partial(kernel, (edge, disp, nodes, padded, tile...  28.7 us
    pallas_call x1, Pallas kernels, on_device(): pl.pallas_call(back_kernel, out_shape=jax.ShapeDtypeStruct((nodes, block,...  17.5 us
    pallas_call x1, Pallas kernels, on_device(): pl.pallas_call(forward_kernel, out_shape=(jax.ShapeDtypeStruct((nodes, ce...  7.87 us
    all_to_all x1, starting transfers between devices, on_device(): lax.all_to_all(middle_buffer, ('gy', 'gz'), split_axis=0, concat_axis=0,...  6.67 us
    pallas_call x1, Pallas kernels, on_device(): pl.pallas_call(final_kernel, out_shape=jax.ShapeDtypeStruct((nodes, 4 * b...  4.46 us
  transfers between devices with their start and end apart: 1, of which 0 were waited for; matrix products, arithmetic and copies ran while one was open for 1% of the time, Pallas kernels for 43%

profile of v5, /device:TPU:17, one launch (start us, length us, event | category | flops | bytes accessed | tf_op | source)
XLA Modules:
  0.0 76.1 jit_solution(6452018575075363393)
XLA Ops:
  0.0 1.0 %slice_bitcast_fusion = f32[2,2,7,4,400]{4,3,1,2,0:T(4,128)S(1)} fusion(f32[2,7,4,3,400]{4,2,3,1,0:T(4,128)} %param.16), kind=kLoop, calls=%fused_computation | loop fusion | bytes 358400 | tf_op jit(solution)/shard_map/transpose | solution.py:235
  1.0 0.8 fusion
  1.8 0.1 mul.22
  1.8 0.3 mul.23
  2.2 0.0 slice-done
  2.2 0.3 squeeze.4
  2.5 0.0 copy-done.1
  2.6 0.3 reshape.37
  2.8 0.3 copy.19
  3.2 0.2 copy.26
  3.4 0.1 mul.24
  3.5 0.9 %pad.9.rest_0_ = f32[2,640,20]{2,1,0:T(8,128)} pad(f32[2,560,20]{2,1,0:T(8,128)S(1)} %mul.24, f32[]{:T(128)} %constant.10.clone.1), padding=0_0x0_80x0_0 | pad | bytes 192004 | tf_op jit(solution)/shard_map/jit(_pad)/pad | solution.py:234
  4.4 0.8 %pad.8.clone = f32[2,4,104,20]{3,2,1,0:T(8,128)} pad(f32[2,4,100,20]{3,2,1,0:T(8,128)S(1)} %copy.26, f32[]{:T(128)} %constant.10.clone.1), padding=0_0x0_0x0_4x0_0 | pad | bytes 130564 | tf_op jit(solution)/shard_map/jit(_pad)/pad | solution.py:390
  5.2 0.1 copy.21
  5.3 0.7 copy.22.rest_1_
  6.0 0.0 copy-done.3
  6.0 0.0 copy-done.2
  6.0 0.6 add.10.dest_ref
  6.6 7.9 %shard_map.145 = (f32[2,400,20]{2,1,0:T(8,128)}, f32[4,2,16,128]{3,2,1,0:T(8,128)}) custom-call(f32[2,416,20]{2,1,0:T(8,128)} %bitcast.19, bf16[2,528,416]{2,1,0:T(8,128)(2,1)} %constant.29.clone.forward_ref.square_ref, f32[20,20]{1,0:T(8,128)} %constant.30.clone.h_ref, f32[16,20]{1,0:T(8,128)} %constant.31.clone.head_ref), custom_call_target="tpu_custom_call" | custom-call | tf_op jit(solution)/shard_map/pallas_call | solution.py:391
  14.5 13.7 %shard_map.146 = f32[32,72,128]{2,1,0:T(8,128)} custom-call(s32[2,7]{1,0:T(2,128)} %add.10.dest_ref, f32[2,400,20]{2,1,0:T(8,128)} %get-tuple-element.9.x_ref, f32[2,640,20]{2,1,0:T(8,128)} %pad.9.rest_0_, f32[2,2,28,400]{3,2,1,0:T(8,128)} %copy.22.rest_1_), custom_call_target="tpu_custom_call" | custom-call | tf_op jit(solution)/shard_map/pallas_call | solution.py:243
  28.2 6.7 %all-to-all-start = ((f32[32,72,128]{2,1,0:T(8,128)}), f32[32,72,128]{2,1,0:T(8,128)S(1)}, u32[]{:S(2)}, u32[]{:S(2)}) async-start(f32[32,72,128]{2,1,0:T(8,128)} %shard_map.146), calls=%async_computation | async-start | bytes 2359296 | tf_op jit(solution)/shard_map/all_to_all | solution.py:414
  34.9 15.0 %shard_map.147 = f32[16,72,128]{2,1,0:T(8,128)} custom-call(s32[2,7]{1,0:T(2,128)} %dest_ref.1, s32[1,8]{1,0:T(1,128)} %place_ref.1, f32[8,16,128]{2,1,0:T(8,128)} %bitcast.22, bf16[2,528,416]{2,1,0:T(8,128)(2,1)} %constant.29.clone.forward_ref.square_ref, f32[2,16,20]{2,1,0:T(8,128)} %constant.32.clone.lane_ref, f32[2,640,20]{2,1,0:T(8,128)} %pad.9.rest_0_, ...), custom_call_target="tpu_custom_call" | custom-call | tf_op jit(solution)/shard_map/pallas_call | solution.py:243
  49.9 0.0 copy-done.4
  49.9 0.6 constant_dynamic-slice_fusion.place_ref
  50.4 17.5 %shard_map.148.parent_ref = f32[2,104,20]{2,1,0:T(8,128)} custom-call(s32[1,2]{1,0:T(1,128)} %constant_dynamic-slice_fusion.place_ref, f32[8,2,72,128]{3,2,1,0:T(8,128)} %bitcast.18, bf16[2,416,432]{2,1,0:T(8,128)(2,1)} %constant.33.clone.inverse_ref, f32[128,20]{1,0:T(8,128)} %constant.34.clone.lane_inverse_ref, f32[2,20,20]{2,1,0:T(8,128)} %constant.35.clone.lane_back_ref), custom_call_target="tpu_custom_call" | custom-call | tf_op jit(solution)/shard_map/pallas_call | solution.py:422
  68.0 0.0 all-to-all-done
  68.0 1.0 %copy-done = f32[32,72,128]{2,1,0:T(8,128)} copy-done((f32[32,72,128]{2,1,0:T(8,128)}, f32[32,72,128]{2,1,0:T(8,128)S(1)}, u32[]{:S(2)}) %copy-start) | copy-done | bytes 1179672
  69.0 4.5 %shard_map.149 = f32[2,416,20]{2,1,0:T(8,128)} custom-call(f32[16,2,72,128]{3,2,1,0:T(8,128)} %bitcast.16, f32[2,104,20]{2,1,0:T(8,128)} %shard_map.148.parent_ref, bf16[2,416,432]{2,1,0:T(8,128)(2,1)} %constant.33.clone.inverse_ref, bf16[2,416,104]{2,1,0:T(8,128)(2,1)} %constant.36.clone.inner_ref, f32[128,20]{1,0:T(8,128)} %constant.34.clone.lane_inverse_ref), custom_call_target="tpu_custom_call" | custom-call | tf_op jit(solution)/shard_map/pallas_call | solution.py:437
  73.5 1.2 %copy.24 = f32[2,416,20]{1,0,2:T(2,128)S(1)} copy(f32[2,416,20]{2,1,0:T(8,128)} %shard_map.149) | data formatting | bytes 133120 | tf_op jit(solution)/shard_map/pallas_call | solution.py:437
  74.7 0.2 reshape.44
  74.8 0.4 copy.25
  75.2 0.9 %reshape.45 = f32[16,1000]{1,0:T(8,128)} reshape(f32[2,4,2,100,10]{4,3,2,1,0:T(8,128)S(1)} %copy.25) | data formatting | bytes 128000 | tf_op jit(solution)/shard_map/reshape | solution.py:448
  (8 shorter events, 0.0 us)
Async XLA Ops:
  0.0 2.2 %slice-start = ((f32[2,7,4,3,400]{4,2,3,1,0:T(4,128)}), f32[2,7,4,1,400]{4,2,3,1,0:T(4,128)S(1)}, s32[]{:S(2)}) async-start(f32[2,7,4,3,400]{4,2,3,1,0:T(4,128)} %param.16), calls=%async_computation.1 | async-start | bytes 229376 | tf_op jit(solution)/shard_map/slice | solution.py:233
  0.0 2.5 %copy-start.1 = (f32[16,1000]{1,0:T(8,128)S(1)}, f32[16,1000]{1,0:T(8,128)}, u32[]{:S(2)}) copy-start(f32[16,1000]{1,0:T(8,128)} %param.15) | copy-start | bytes 192004
  4.4 1.7 %copy-start.3 = (s32[2,7,1]{1,2,0:T(1,128)S(1)}, s32[2,7,1]{1,2,0:T(1,128)}, u32[]{:S(2)}) copy-start(s32[2,7,1]{1,2,0:T(1,128)} %param.18) | copy-start | bytes 172
  4.4 1.7 %copy-start.2 = (s32[2,7]{1,0:T(2,128)S(1)}, s32[2,7]{1,0:T(2,128)}, u32[]{:S(2)}) copy-start(s32[2,7]{1,0:T(2,128)} %param.19) | copy-start | bytes 172
  28.2 39.8 %all-to-all-start = ((f32[32,72,128]{2,1,0:T(8,128)}), f32[32,72,128]{2,1,0:T(8,128)S(1)}, u32[]{:S(2)}, u32[]{:S(2)}) async-start(f32[32,72,128]{2,1,0:T(8,128)} %shard_map.146), calls=%async_computation | async-start | bytes 2359296 | tf_op jit(solution)/shard_map/all_to_all | solution.py:414
  34.9 15.0 %copy-start.4 = (s32[1,8]{1,0:T(1,128)S(1)}, s32[1,8]{1,0:T(1,128)}, u32[]{:S(2)}) copy-start(s32[1,8]{1,0:T(1,128)} %place_ref.1) | copy-start | bytes 100
  68.0 1.0 %copy-start = (f32[32,72,128]{2,1,0:T(8,128)}, f32[32,72,128]{2,1,0:T(8,128)S(1)}, u32[]{:S(2)}) copy-start(f32[32,72,128]{2,1,0:T(8,128)S(1)} %all-to-all-done) | copy-start | bytes 3538948

commit v6 on v5

--- a/solution.py
+++ b/solution.py
@@ -107,10 +107,8 @@
     ).astype(jnp.bfloat16)
 
     def fill(slot, value):
-        high = value.astype(jnp.bfloat16)
-        rest = value - high.astype(jnp.float32)
-        mid, low = halves(rest)
-        table = tn_dot(high, spread) + tn_dot(mid, spread) + tn_dot(low, spread)
+        high, low = halves(value)
+        table = tn_dot(high, spread) + tn_dot(low, spread)
         for tile in range(tiles):
             coef_ref[slot, tile] = table[:, tile * LANES:(tile + 1) * LANES]
 
@@ -129,7 +127,7 @@
             else:
                 ping_ref[tile, at, :] = jnp.zeros((cells, LANES), jnp.float32)
 
-    group = 4
+    group = 5
     groups = edge // group
 
     def contract(slot, source_ref, target_ref):

time: 76.5 us -> 75.4 us (0.986)
  Pallas kernels: 58.5 us -> 57.5 us
    pallas_call x2, Pallas kernels: 28.7 us -> 27.6 us  [images(): pl.pallas_call(functools.partial(kernel, (edge, disp, nodes, padded, tile...]
where the time goes in v6:
time: 75.4 us; the launch traced here: 75 us
  Pallas kernels  57.5 us (76%)
  local copies, waits for them, and re-layouts  9.39 us (12%)
  starting transfers between devices  6.66 us (9%)
  other arithmetic  1.38 us (2%)
    pallas_call x2, Pallas kernels, images(): pl.pallas_call(functools.partial(kernel, (edge, disp, nodes, padded, tile...  27.6 us
    pallas_call x1, Pallas kernels, on_device(): pl.pallas_call(back_kernel, out_shape=jax.ShapeDtypeStruct((nodes, block,...  17.6 us
    pallas_call x1, Pallas kernels, on_device(): pl.pallas_call(forward_kernel, out_shape=(jax.ShapeDtypeStruct((nodes, ce...  7.87 us
    all_to_all x1, starting transfers between devices, on_device(): lax.all_to_all(middle_buffer, ('gy', 'gz'), split_axis=0, concat_axis=0,...  6.66 us
    pallas_call x1, Pallas kernels, on_device(): pl.pallas_call(final_kernel, out_shape=jax.ShapeDtypeStruct((nodes, 4 * b...  4.46 us
  transfers between devices with their start and end apart: 1, of which 0 were waited for; matrix products, arithmetic and copies ran while one was open for 1% of the time, Pallas kernels for 43%

profile of v6, /device:TPU:17, one launch (start us, length us, event | category | flops | bytes accessed | tf_op | source)
XLA Modules:
  0.0 75.0 jit_solution(10494398327415508755)
XLA Ops:
  0.0 1.0 %slice_bitcast_fusion = f32[2,2,7,4,400]{4,3,1,2,0:T(4,128)S(1)} fusion(f32[2,7,4,3,400]{4,2,3,1,0:T(4,128)} %param.16), kind=kLoop, calls=%fused_computation | loop fusion | bytes 358400 | tf_op jit(solution)/shard_map/transpose | solution.py:233
  1.0 0.8 %fusion = f32[2,7,4]{2,1,0:T(8,128)S(1)} fusion(s32[2,7]{1,0:T(2,128)} %param.17), kind=kLoop, calls=%fused_computation.3 | loop fusion | flops 112 | bytes 280 | tf_op jit(solution)/shard_map/convert_element_type | solution.py:230
  1.8 0.1 mul.22
  1.8 0.3 mul.23
  2.2 0.0 slice-done
  2.2 0.3 squeeze.4
  2.5 0.0 copy-done.1
  2.6 0.3 reshape.37
  2.8 0.3 copy.19
  3.2 0.2 copy.26
  3.4 0.1 mul.24
  3.5 0.9 %pad.9.rest_0_ = f32[2,640,20]{2,1,0:T(8,128)} pad(f32[2,560,20]{2,1,0:T(8,128)S(1)} %mul.24, f32[]{:T(128)} %constant.10.clone.1), padding=0_0x0_80x0_0 | pad | bytes 192004 | tf_op jit(solution)/shard_map/jit(_pad)/pad | solution.py:232
  4.4 0.8 %pad.8.clone = f32[2,4,104,20]{3,2,1,0:T(8,128)} pad(f32[2,4,100,20]{3,2,1,0:T(8,128)S(1)} %copy.26, f32[]{:T(128)} %constant.10.clone.1), padding=0_0x0_0x0_4x0_0 | pad | bytes 130564 | tf_op jit(solution)/shard_map/jit(_pad)/pad | solution.py:388
  5.2 0.1 copy.21
  5.3 0.7 copy.22.rest_1_
  6.0 0.0 copy-done.3
  6.0 0.0 copy-done.2
  6.0 0.6 add.10.dest_ref
  6.6 7.9 %shard_map.145 = (f32[2,400,20]{2,1,0:T(8,128)}, f32[4,2,16,128]{3,2,1,0:T(8,128)}) custom-call(f32[2,416,20]{2,1,0:T(8,128)} %bitcast.19, bf16[2,528,416]{2,1,0:T(8,128)(2,1)} %constant.29.clone.forward_ref.square_ref, f32[20,20]{1,0:T(8,128)} %constant.30.clone.h_ref, f32[16,20]{1,0:T(8,128)} %constant.31.clone.head_ref), custom_call_target="tpu_custom_call" | custom-call | tf_op jit(solution)/shard_map/pallas_call | solution.py:389
  14.5 13.1 %shard_map.146 = f32[32,72,128]{2,1,0:T(8,128)} custom-call(s32[2,7]{1,0:T(2,128)} %add.10.dest_ref, f32[2,400,20]{2,1,0:T(8,128)} %get-tuple-element.9.x_ref, f32[2,640,20]{2,1,0:T(8,128)} %pad.9.rest_0_, f32[2,2,28,400]{3,2,1,0:T(8,128)} %copy.22.rest_1_), custom_call_target="tpu_custom_call" | custom-call | tf_op jit(solution)/shard_map/pallas_call | solution.py:241
  27.6 6.7 %all-to-all-start = ((f32[32,72,128]{2,1,0:T(8,128)}), f32[32,72,128]{2,1,0:T(8,128)S(1)}, u32[]{:S(2)}, u32[]{:S(2)}) async-start(f32[32,72,128]{2,1,0:T(8,128)} %shard_map.146), calls=%async_computation | async-start | bytes 2359296 | tf_op jit(solution)/shard_map/all_to_all | solution.py:412
  34.3 14.5 %shard_map.147 = f32[16,72,128]{2,1,0:T(8,128)} custom-call(s32[2,7]{1,0:T(2,128)} %dest_ref.1, s32[1,8]{1,0:T(1,128)} %place_ref.1, f32[8,16,128]{2,1,0:T(8,128)} %bitcast.22, bf16[2,528,416]{2,1,0:T(8,128)(2,1)} %constant.29.clone.forward_ref.square_ref, f32[2,16,20]{2,1,0:T(8,128)} %constant.32.clone.lane_ref, f32[2,640,20]{2,1,0:T(8,128)} %pad.9.rest_0_, ...), custom_call_target="tpu_custom_call" | custom-call | tf_op jit(solution)/shard_map/pallas_call | solution.py:241
  48.7 0.6 constant_dynamic-slice_fusion.place_ref
  49.3 17.6 %shard_map.148.parent_ref = f32[2,104,20]{2,1,0:T(8,128)} custom-call(s32[1,2]{1,0:T(1,128)} %constant_dynamic-slice_fusion.place_ref, f32[8,2,72,128]{3,2,1,0:T(8,128)} %bitcast.18, bf16[2,416,432]{2,1,0:T(8,128)(2,1)} %constant.33.clone.inverse_ref, f32[128,20]{1,0:T(8,128)} %constant.34.clone.lane_inverse_ref, f32[2,20,20]{2,1,0:T(8,128)} %constant.35.clone.lane_back_ref), custom_call_target="tpu_custom_call" | custom-call | tf_op jit(solution)/shard_map/pallas_call | solution.py:420
  66.9 0.0 all-to-all-done
  66.9 0.0 copy-start
  66.9 1.0 %copy-done = f32[32,72,128]{2,1,0:T(8,128)} copy-done((f32[32,72,128]{2,1,0:T(8,128)}, f32[32,72,128]{2,1,0:T(8,128)S(1)}, u32[]{:S(2)}) %copy-start) | copy-done | bytes 1179672
  67.9 4.5 %shard_map.149 = f32[2,416,20]{2,1,0:T(8,128)} custom-call(f32[16,2,72,128]{3,2,1,0:T(8,128)} %bitcast.16, f32[2,104,20]{2,1,0:T(8,128)} %shard_map.148.parent_ref, bf16[2,416,432]{2,1,0:T(8,128)(2,1)} %constant.33.clone.inverse_ref, bf16[2,416,104]{2,1,0:T(8,128)(2,1)} %constant.36.clone.inner_ref, f32[128,20]{1,0:T(8,128)} %constant.34.clone.lane_inverse_ref), custom_call_target="tpu_custom_call" | custom-call | tf_op jit(solution)/shard_map/pallas_call | solution.py:435
  72.4 1.2 %copy.24 = f32[2,416,20]{1,0,2:T(2,128)S(1)} copy(f32[2,416,20]{2,1,0:T(8,128)} %shard_map.149) | data formatting | bytes 133120 | tf_op jit(solution)/shard_map/pallas_call | solution.py:435
  73.6 0.2 reshape.44
  73.8 0.4 copy.25
  74.1 0.9 %reshape.45 = f32[16,1000]{1,0:T(8,128)} reshape(f32[2,4,2,100,10]{4,3,2,1,0:T(8,128)S(1)} %copy.25) | data formatting | bytes 128000 | tf_op jit(solution)/shard_map/reshape | solution.py:446
  (8 shorter events, 0.0 us)
Async XLA Ops:
  0.0 2.2 %slice-start = ((f32[2,7,4,3,400]{4,2,3,1,0:T(4,128)}), f32[2,7,4,1,400]{4,2,3,1,0:T(4,128)S(1)}, s32[]{:S(2)}) async-start(f32[2,7,4,3,400]{4,2,3,1,0:T(4,128)} %param.16), calls=%async_computation.1 | async-start | bytes 229376 | tf_op jit(solution)/shard_map/slice | solution.py:231
  0.0 2.5 %copy-start.1 = (f32[16,1000]{1,0:T(8,128)S(1)}, f32[16,1000]{1,0:T(8,128)}, u32[]{:S(2)}) copy-start(f32[16,1000]{1,0:T(8,128)} %param.15) | copy-start | bytes 192004
  4.4 1.7 %copy-start.3 = (s32[2,7,1]{1,2,0:T(1,128)S(1)}, s32[2,7,1]{1,2,0:T(1,128)}, u32[]{:S(2)}) copy-start(s32[2,7,1]{1,2,0:T(1,128)} %param.18) | copy-start | bytes 172
  4.4 1.7 %copy-start.2 = (s32[2,7]{1,0:T(2,128)S(1)}, s32[2,7]{1,0:T(2,128)}, u32[]{:S(2)}) copy-start(s32[2,7]{1,0:T(2,128)} %param.19) | copy-start | bytes 172
  27.6 39.3 %all-to-all-start = ((f32[32,72,128]{2,1,0:T(8,128)}), f32[32,72,128]{2,1,0:T(8,128)S(1)}, u32[]{:S(2)}, u32[]{:S(2)}) async-start(f32[32,72,128]{2,1,0:T(8,128)} %shard_map.146), calls=%async_computation | async-start | bytes 2359296 | tf_op jit(solution)/shard_map/all_to_all | solution.py:412
  34.3 14.5 %copy-start.4 = (s32[1,8]{1,0:T(1,128)S(1)}, s32[1,8]{1,0:T(1,128)}, u32[]{:S(2)}) copy-start(s32[1,8]{1,0:T(1,128)} %place_ref.1) | copy-start | bytes 100
  66.9 1.0 %copy-start = (f32[32,72,128]{2,1,0:T(8,128)}, f32[32,72,128]{2,1,0:T(8,128)S(1)}, u32[]{:S(2)}) copy-start(f32[32,72,128]{2,1,0:T(8,128)S(1)} %all-to-all-done) | copy-start | bytes 3538948
